TPU v7x, 128 devices: a whole 4x4x4 slice. The times are simulated.
128 devices in a mesh: gx: 8 (over y, core), gy: 16 (over z, x).
Axes of the slice: x: 4, y: 4, z: 4, core: 2. Of those that a mesh axis runs over, the one named last changes fastest.
Arguments:
- model_state: float32 [200, 256, 2048], P(None, 'gx', 'gy'), may hold values from -6 to 6
- obs_cell: int32 [128, 2048], P(('gx', 'gy')), may hold values from 0 to 4095
- obs_count: int32 [128, 128], P(('gx', 'gy')), may hold values from 0 to 16, as said below
- obs_value: float32 [16, 262144], P(None, ('gx', 'gy')), may hold values from -6 to 6
- obs_weight: float32 [16, 262144], P(None, ('gx', 'gy')), may hold values from 0.25 to 4
- predictor: float32 [8, 262144], P(None, ('gx', 'gy')), may hold values from -6 to 6
- bias_coef: float32 [16, 8], replicated, may hold values from -3 to 3
- weight_in: float32 [768, 200], replicated, may hold values from -0.4375 to 0.4375
- bias_in: float32 [768], replicated, may hold values from -3 to 3
- weight_mid: float32 [768, 768], replicated, may hold values from -0.21875 to 0.21875
- bias_mid: float32 [768], replicated, may hold values from -3 to 3
- weight_out: float32 [16, 768], replicated, may hold values from -0.21875 to 0.21875
- bias_out: float32 [16], replicated, may hold values from -4 to 4
Outputs:
- gradient: float32 [200, 256, 2048], P(None, 'gx', 'gy')
- evolved: float32 [16, 262144], P(None, ('gx', 'gy'))
- bias_gradient: float32 [16, 8], replicated
Inputs may be any that keep to these rules, and one draw needn't show every extreme that they name: obs_count[o, s] is how many of the 16 slots that owner o keeps for grid block s are used, from the first on; for some block s every owner uses all 16. `obs_cell`: a cell within a block is numbered row within the block times 128 plus column within the block.
All inputs are finite; a program needn't handle non-finite values.
Results may differ from a plain program's by a relative error of at most 0.000096.
Values sent between devices are 32-bit elements; how exact they have to be, the bound alone decides.
No kernel may reach another device: no remote copies, remote signals or barrier semaphores. Data moves between devices by JAX's collectives and lax.ppermute only.
A program may use at most 64 MiB of HBM per device.

v0:
```python
import jax
import jax.numpy as jnp
from jax import lax
from jax.sharding import PartitionSpec as P


def product(lhs_array, rhs_array):
    return jnp.dot(
        lhs_array, rhs_array, preferred_element_type=jnp.float32, precision=lax.Precision.HIGHEST
    )


def observe(
    profile,
    obs_rows,
    weight_rows,
    pred_rows,
    bias_coef,
    weight_in,
    bias_in,
    weight_mid,
    bias_mid,
    weight_out,
    bias_out,
):
    hidden_in = jnp.tanh(product(weight_in, profile) + bias_in[:, None])
    hidden_mid = jnp.tanh(product(weight_mid, hidden_in) + bias_mid[:, None])
    model_out = product(weight_out, hidden_mid) + bias_out[:, None] + product(bias_coef, pred_rows)
    residual_term = weight_rows * (model_out - obs_rows)
    back_mid = product(weight_out.T, residual_term) * (1.0 - hidden_mid * hidden_mid)
    back_in = product(weight_mid.T, back_mid) * (1.0 - hidden_in * hidden_in)
    increment = product(weight_in.T, back_in)
    bias_part = product(residual_term, pred_rows.T)
    return (model_out, increment, bias_part)


def exchange_blocks(block_data):
    return lax.all_to_all(block_data, ("gx", "gy"), split_axis=1, concat_axis=1, tiled=True)


def per_device(
    model_state,
    obs_cell,
    obs_count,
    obs_value,
    obs_weight,
    predictor,
    bias_coef,
    weight_in,
    bias_in,
    weight_mid,
    bias_mid,
    weight_out,
    bias_out,
):
    groups_x = lax.axis_size("gx")
    devices = groups_x * lax.axis_size("gy")
    features, block_rows, block_cols = model_state.shape
    slot_total = obs_cell.shape[1]
    capacity = slot_total // devices
    asked_cells = lax.all_to_all(obs_cell, ("gx", "gy"), split_axis=1, concat_axis=1, tiled=True)[0]
    columns = jnp.take(model_state.reshape(features, block_rows * block_cols), asked_cells, axis=1)
    valid_slot = (jnp.arange(capacity, dtype=jnp.int32)[None, :] < obs_count[0][:, None]).reshape(
        slot_total
    )
    masked_weight = jnp.where(valid_slot[None, :], obs_weight, jnp.float32(0.0))
    profile = exchange_blocks(columns)
    model_out, increment, bias_part = observe(
        profile,
        obs_value,
        masked_weight,
        predictor,
        bias_coef,
        weight_in,
        bias_in,
        weight_mid,
        bias_mid,
        weight_out,
        bias_out,
    )
    returned = exchange_blocks(increment)
    gradient = (
        jnp.zeros((features, block_rows * block_cols), jnp.float32).at[:, asked_cells].add(returned)
    )
    bias_gradient = lax.psum(bias_part, ("gx", "gy"))
    evolved = jnp.where(valid_slot[None, :], model_out, jnp.float32(0.0))
    return (gradient.reshape(features, block_rows, block_cols), evolved, bias_gradient)


def solution(mesh):
    in_specs = (
        P(None, "gx", "gy"),
        P(("gx", "gy"), None),
        P(("gx", "gy"), None),
        P(None, ("gx", "gy")),
        P(None, ("gx", "gy")),
        P(None, ("gx", "gy")),
        P(),
        P(),
        P(),
        P(),
        P(),
        P(),
        P(),
    )
    out_specs = (P(None, "gx", "gy"), P(None, ("gx", "gy")), P())
    return jax.shard_map(
        per_device, mesh=mesh, in_specs=in_specs, out_specs=out_specs, check_vma=False
    )
```

profile of v0, /device:TPU:1, one launch (start us, length us, event | category | flops | bytes accessed | tf_op | source)
XLA Modules:
  0.0 247.6 jit_solution(6036368607073711215)
XLA Ops:
  0.6 0.0 copy-start
  0.6 0.5 broadcast.68
  1.2 1.6 reduce.6
  2.7 0.7 all_to_all.20
  3.4 11.5 %all-to-all-start = ((s32[1,128,16]{2,0,1:T(1,128)}), s32[1,128,16]{2,0,1:T(1,128)S(1)}, u32[]{:S(2)}, u32[]{:S(2)}) async-start(s32[1,128,16]{2,0,1:T(1,128)} %bitcast), calls=%async_computation | async-start | bytes 131072 | tf_op jit(solution)/shard_map/all_to_all | solution.py:61
  14.9 5.0 %copy.23 = f32[200,32,128]{0,2,1:T(8,128)} copy(f32[200,32,128]{2,1,0:T(8,128)} %param.13) | data formatting | bytes 6553600 | tf_op args[0]
  20.0 4.7 %all-to-all-done = s32[1,128,16]{2,0,1:T(1,128)S(1)} async-done(((s32[1,128,16]{2,0,1:T(1,128)}), s32[1,128,16]{2,0,1:T(1,128)S(1)}, u32[]{:S(2)}, u32[]{:S(2)}) %all-to-all-start) | async-done | bytes 8224 | tf_op jit(solution)/shard_map/all_to_all | solution.py:61
  24.7 0.8 reduce.7
  25.5 0.1 squeeze.5
  25.6 10.8 %gather_fusion = f32[2048,200]{1,0:T(8,128)} fusion(f32[200,4096]{0,1:T(8,128)} %bitcast.31, s32[2048]{0:T(1024)S(1)} %broadcast_clamp_fusion), kind=kCustom, calls=%fused_computation | custom fusion | bytes 3284992 | tf_op jit(solution)/shard_map/jit(_take)/gather | solution.py:62
  36.4 0.0 copy-start.10
  36.4 3.3 %broadcast_select_fusion = f32[200,128,16]{0,2,1:T(8,128)} fusion(f32[200,128,16]{0,2,1:T(8,128)} %bitcast.34, pred[128,16]{1,0:T(8,128)(4,1)S(1)} %compare_and_fusion), kind=kLoop, calls=%fused_computation.26 | loop fusion | flops 409600 | bytes 3278848 | tf_op jit(solution)/shard_map/jit(_take)/select_n | solution.py:62
  39.7 6.1 %all-to-all-start.1 = ((f32[200,128,16]{0,2,1:T(8,128)}), f32[200,128,16]{0,2,1:T(8,128)}, u32[]{:S(2)}, u32[]{:S(2)}) async-start(f32[200,128,16]{0,2,1:T(8,128)} %broadcast_select_fusion), calls=%async_computation.1 | async-start | bytes 4194304 | tf_op jit(solution)/shard_map/all_to_all | solution.py:38
  45.8 0.0 copy-done.10
  45.8 0.1 iota_compare_fusion
  45.9 0.1 lt.52
  46.0 28.3 %all-to-all-done.1 = f32[200,128,16]{0,2,1:T(8,128)} async-done(((f32[200,128,16]{0,2,1:T(8,128)}), f32[200,128,16]{0,2,1:T(8,128)}, u32[]{:S(2)}, u32[]{:S(2)}) %all-to-all-start.1) | async-done | bytes 1638432 | tf_op jit(solution)/shard_map/all_to_all | solution.py:38
  74.3 0.0 copy-done.1
  74.3 7.5 %fusion.25 = f32[2048,768]{1,0:T(8,128)S(1)} fusion(f32[200,2048]{0,1:T(8,128)} %bitcast.7, f32[768,200]{0,1:T(8,128)S(1)} %copy-done.1), kind=kOutput, calls=%fused_computation.36 | convolution fusion | flops 3774873600 | bytes 8544256 | tf_op jit(solution)/shard_map/dot_general | solution.py:8
  81.8 0.0 copy-done
  81.8 0.0 copy-done.8
  81.8 0.0 copy-start.3
  81.8 0.0 copy-start.6
  81.8 0.0 copy-start.9
  81.8 17.4 %fusion.8 = f32[2048,768]{1,0:T(8,128)S(1)} fusion(f32[768,768]{1,0:T(8,128)S(1)} %copy-done, f32[2048,768]{1,0:T(8,128)S(1)} %fusion.25, f32[768]{0:T(1024)S(1)} %copy-done.8), kind=kOutput, calls=%fused_computation.12 | convolution fusion | flops 14497087488 | bytes 14945280 | tf_op jit(solution)/shard_map/dot_general | solution.py:8
  99.3 0.0 copy-done.3
  99.3 0.0 copy-done.6
  99.3 0.0 copy-done.9
  99.3 0.0 copy-start.2
  99.3 0.0 copy-start.4
  99.3 0.0 copy-start.5
  99.4 0.0 copy-start.7
  99.4 6.0 %fusion.20 = f32[16,2048]{1,0:T(8,128)S(1)} fusion(f32[16,768]{1,0:T(8,128)S(1)} %copy-done.3, f32[2048,768]{1,0:T(8,128)S(1)} %fusion.8, f32[768]{0:T(1024)S(1)} %copy-done.6, f32[16]{0:T(128)S(1)} %copy-done.9), kind=kOutput, calls=%fused_computation.23 | convolution fusion | flops 303595520 | bytes 6474816 | tf_op jit(solution)/shard_map/dot_general | solution.py:8
  105.3 0.0 copy-done.2
  105.3 0.0 copy-done.4
  105.3 0.0 copy-done.5
  105.4 0.0 copy-done.7
  105.4 1.0 broadcast_select_fusion.1
  106.4 5.3 %fusion.26 = f32[2048,768]{1,0:T(8,128)S(1)} fusion(f32[16,2048]{1,0:T(8,128)S(1)} %get-tuple-element.13, f32[16,768]{1,0:T(8,128)S(1)} %copy-done.3), kind=kOutput, calls=%fused_computation.37 | convolution fusion | flops 301989888 | bytes 6471680 | tf_op jit(solution)/shard_map/dot_general | solution.py:8
  111.7 17.5 %fusion.2 = f32[2048,768]{1,0:T(8,128)S(1)} fusion(f32[768,768]{1,0:T(8,128)S(1)} %copy-done, f32[2048,768]{1,0:T(8,128)S(1)} %fusion.26, f32[2048,768]{1,0:T(8,128)S(1)} %fusion.8, f32[768]{0:T(1024)S(1)} %copy-done.6), kind=kOutput, calls=%fused_computation.4 | convolution fusion | flops 14501806080 | bytes 21236736 | tf_op jit(solution)/shard_map/dot_general | solution.py:8
  129.1 8.9 %fusion.16 = f32[200,2048]{1,0:T(8,128)} fusion(f32[768,200]{0,1:T(8,128)S(1)} %copy-done.1, f32[2048,768]{1,0:T(8,128)S(1)} %fusion.2, f32[2048,768]{1,0:T(8,128)S(1)} %fusion.25, f32[768]{0:T(1024)S(1)} %copy-done.8), kind=kOutput, calls=%fused_computation.20 | convolution fusion | flops 3781165056 | bytes 14838784 | tf_op jit(solution)/shard_map/dot_general | solution.py:8
  138.0 2.8 %copy.24 = f32[200,2048]{0,1:T(8,128)} copy(f32[200,2048]{1,0:T(8,128)} %fusion.16) | data formatting | bytes 3276800 | tf_op jit(solution)/shard_map/dot_general | solution.py:8
  140.8 6.1 %all-to-all-start.2 = ((f32[200,128,16]{0,2,1:T(8,128)}), f32[200,128,16]{0,2,1:T(8,128)}, u32[]{:S(2)}, u32[]{:S(2)}) async-start(f32[200,128,16]{0,2,1:T(8,128)} %bitcast.33), calls=%async_computation.2 | async-start | bytes 4194304 | tf_op jit(solution)/shard_map/all_to_all | solution.py:38
  146.9 0.2 fusion.27
  147.1 81.2 %psum.7 = f32[16,8]{0,1:T(8,128)} all-reduce(f32[16,8]{0,1:T(8,128)S(1)} %fusion.27), channel_id=1, replica_groups=mesh['gx'=8,'gy'=16] {'gx','gy'}, use_global_device_ids=true, to_apply=%region_1.2 | all-reduce | flops 128 | bytes 1024 | tf_op jit(solution)/shard_map/psum | solution.py:85
  228.3 0.0 all-to-all-done.2
  228.3 14.1 %scatter_custom_fusion = f32[200,4096]{0,1:T(8,128)} fusion(s32[2048]{0:T(1024)S(1)} %bitcast.37, f32[2048,200]{1,0:T(8,128)} %bitcast.12, f32[]{:T(128)} %constant.6.clone.1), kind=kCustom, calls=%fused_computation.24 | custom fusion | flops 409600 | bytes 3277312 | tf_op jit(solution)/shard_map/scatter-add | solution.py:83
  242.4 5.0 %copy.25 = f32[200,32,128]{2,1,0:T(8,128)} copy(f32[200,32,128]{0,2,1:T(8,128)} %bitcast.32) | data formatting | bytes 6553600
  (5 shorter events, 0.0 us)
Async XLA Ops:
  0.6 81.2 %copy-start = (f32[768,768]{1,0:T(8,128)S(1)}, f32[768,768]{1,0:T(8,128)}, u32[]{:S(2)}) copy-start(f32[768,768]{1,0:T(8,128)} %param.22) | copy-start | bytes 7077892
  3.4 21.2 %all-to-all-start = ((s32[1,128,16]{2,0,1:T(1,128)}), s32[1,128,16]{2,0,1:T(1,128)S(1)}, u32[]{:S(2)}, u32[]{:S(2)}) async-start(s32[1,128,16]{2,0,1:T(1,128)} %bitcast), calls=%async_computation | async-start | bytes 131072 | tf_op jit(solution)/shard_map/all_to_all | solution.py:61
  36.4 9.4 %copy-start.10 = (s32[1,128]{1,0:T(1,128)S(1)}, s32[1,128]{1,0:T(1,128)}, u32[]{:S(2)}) copy-start(s32[1,128]{1,0:T(1,128)} %param.15) | copy-start | bytes 1540
  36.4 37.9 %copy-start.1 = (f32[768,200]{0,1:T(8,128)S(1)}, f32[768,200]{0,1:T(8,128)}, u32[]{:S(2)}) copy-start(f32[768,200]{0,1:T(8,128)} %param.20) | copy-start | bytes 1843204
  39.7 34.6 %all-to-all-start.1 = ((f32[200,128,16]{0,2,1:T(8,128)}), f32[200,128,16]{0,2,1:T(8,128)}, u32[]{:S(2)}, u32[]{:S(2)}) async-start(f32[200,128,16]{0,2,1:T(8,128)} %broadcast_select_fusion), calls=%async_computation.1 | async-start | bytes 4194304 | tf_op jit(solution)/shard_map/all_to_all | solution.py:38
  74.3 7.5 %copy-start.8 = (f32[768]{0:T(1024)S(1)}, f32[768]{0:T(1024)}, u32[]{:S(2)}) copy-start(f32[768]{0:T(1024)} %param.21) | copy-start | bytes 9220
  81.8 17.5 %copy-start.3 = (f32[16,768]{1,0:T(8,128)S(1)}, f32[16,768]{1,0:T(8,128)}, u32[]{:S(2)}) copy-start(f32[16,768]{1,0:T(8,128)} %param.24) | copy-start | bytes 147460
  81.8 17.5 %copy-start.6 = (f32[768]{0:T(1024)S(1)}, f32[768]{0:T(1024)}, u32[]{:S(2)}) copy-start(f32[768]{0:T(1024)} %param.23) | copy-start | bytes 9220
  81.8 17.5 %copy-start.9 = (f32[16]{0:T(128)S(1)}, f32[16]{0:T(128)}, u32[]{:S(2)}) copy-start(f32[16]{0:T(128)} %param.25) | copy-start | bytes 196
  99.3 6.0 %copy-start.2 = (f32[8,2048]{1,0:T(8,128)S(1)}, f32[8,2048]{1,0:T(8,128)}, u32[]{:S(2)}) copy-start(f32[8,2048]{1,0:T(8,128)} %param.18) | copy-start | bytes 196612
  99.3 6.0 %copy-start.4 = (f32[16,2048]{1,0:T(8,128)S(1)}, f32[16,2048]{1,0:T(8,128)}, u32[]{:S(2)}) copy-start(f32[16,2048]{1,0:T(8,128)} %param.16) | copy-start | bytes 393220
  99.3 6.0 %copy-start.5 = (f32[16,2048]{1,0:T(8,128)S(1)}, f32[16,2048]{1,0:T(8,128)}, u32[]{:S(2)}) copy-start(f32[16,2048]{1,0:T(8,128)} %param.17) | copy-start | bytes 393220
  99.4 6.0 %copy-start.7 = (f32[16,8]{0,1:T(8,128)S(1)}, f32[16,8]{0,1:T(8,128)}, u32[]{:S(2)}) copy-start(f32[16,8]{0,1:T(8,128)} %param.19) | copy-start | bytes 1540
  140.8 87.5 %all-to-all-start.2 = ((f32[200,128,16]{0,2,1:T(8,128)}), f32[200,128,16]{0,2,1:T(8,128)}, u32[]{:S(2)}, u32[]{:S(2)}) async-start(f32[200,128,16]{0,2,1:T(8,128)} %bitcast.33), calls=%async_computation.2 | async-start | bytes 4194304 | tf_op jit(solution)/shard_map/all_to_all | solution.py:38
where the time goes:
time: 251 us; the launch traced here: 248 us
  blocking collectives  81.2 us (32%)
  matrix products  63.7 us (25%)
  waiting for transfers between devices  33 us (13%)
  local copies, waits for them, and re-layouts  25.1 us (10%)
  starting transfers between devices  23.6 us (9%)
  other arithmetic  19.9 us (8%)
    psum x1, blocking collectives, per_device(): bias_gradient = lax.psum(bias_part, ('gx', 'gy'))  81.2 us
    dot_general x8, matrix products, product(): jnp.dot(lhs_array, rhs_array, preferred_element_type=jnp.float32, precisi...  63.7 us
    all_to_all x2, waiting for transfers between devices, exchange_blocks(): lax.all_to_all(block_data, ('gx', 'gy'), split_axis=1, concat_axis=1, til...  28.3 us
    scatter-add x1, other arithmetic, per_device(): jnp.zeros((features, block_rows * block_cols), jnp.float32)  14.1 us
    all_to_all x2, starting transfers between devices, exchange_blocks(): lax.all_to_all(block_data, ('gx', 'gy'), split_axis=1, concat_axis=1, til...  12.1 us
    all_to_all x1, starting transfers between devices, per_device(): lax.all_to_all(obs_cell, ('gx', 'gy'), split_axis=1, concat_axis=1, tiled...  11.5 us
    gather x1, local copies, waits for them, and re-layouts, per_device(): jnp.take(model_state.reshape(features, block_rows * block_cols), asked_ce...  10.8 us
    unnamed x25, local copies, waits for them, and re-layouts  10.6 us
  transfers between devices with their start and end apart: 3, of which 2 were waited for; matrix products, arithmetic and copies ran while one was open for 2% of the time, Pallas kernels for 0%

commit v1 on v0

v1 whole, which is shorter than its diff:
```python
import functools

import jax
import jax.numpy as jnp
from jax import lax
from jax.experimental import pallas as pl
from jax.experimental.pallas import tpu as pltpu
from jax.sharding import PartitionSpec as P

F32 = jnp.float32
BF16 = jnp.bfloat16
LANES = 128
GROUP = 16
TILE = 512


def split(x):
    high = x.astype(BF16)
    return high, (x - high.astype(F32)).astype(BF16)


def mm(lhs, rhs):
    return jnp.dot(lhs, rhs, preferred_element_type=F32)


def mm3(lhs, rhs_high, rhs_low):
    high, low = split(lhs)
    return mm(high, rhs_high) + (mm(low, rhs_high) + mm(high, rhs_low))


def swap_groups(x):
    rows = x.shape[0]
    differ = lax.broadcasted_iota(jnp.int32, x.shape, 0) ^ (
        lax.broadcasted_iota(jnp.int32, x.shape, 1) // GROUP
    )
    group = lax.broadcasted_iota(jnp.int32, x.shape, 1) // GROUP
    for bit in (1, 2, 4):
        up = pltpu.roll(pltpu.roll(x, rows - bit, 0), GROUP * bit, 1)
        down = pltpu.roll(pltpu.roll(x, bit, 0), LANES - GROUP * bit, 1)
        moved = jnp.where((group & bit) != 0, up, down)
        x = jnp.where((differ & bit) == 0, x, moved)
    return x


def to_tiles(arrays):
    return jnp.concatenate(
        [a[:, i : i + LANES] for a in arrays for i in range(0, a.shape[1], LANES)], axis=0
    )


def used_slots(count_ref):
    peers = count_ref.shape[1]
    counts = jnp.broadcast_to(count_ref[...].astype(F32), (peers, peers)).T
    slot = lax.broadcasted_iota(jnp.int32, (peers, LANES), 1) % GROUP
    return slot.astype(F32) < counts


def request_kernel(cell, count, obs, weight, pred, coef, bias, send, base):
    peers = count.shape[1]
    linear = jnp.broadcast_to(bias[...], obs.shape)
    for i in range(pred.shape[0]):
        linear = linear + coef[:, i : i + 1] * pred[i : i + 1, :]
    base[...] = linear
    target = obs[...] - linear
    cells = jnp.broadcast_to(cell[...].astype(F32), (8, cell.shape[1]))
    packed = swap_groups(
        to_tiles([target[:8], target[8:], weight[:8, :], weight[8:, :], pred[...], cells])
    )
    used = used_slots(count)
    for a in range(6):
        rows = packed[a * peers : (a + 1) * peers]
        if a in (2, 3):
            rows = jnp.where(used, rows, 0.0)
        send[pl.ds(a, peers, stride=8), :] = rows


def prepare_kernel(state, w_in_t, w_mid, w_out, s0, s1, wi_f, wi_b, wm_f, wm_b, wo_f, wo_b):
    feat, rows, cols = 200, 32, 128
    hid = w_mid.shape[0]
    fill = jnp.zeros((256 - feat, cols), F32)
    for r in range(rows):
        block = jnp.concatenate([state[pl.ds(r, feat, stride=rows), :], fill], axis=0)
        turned = block.T
        s0[r * cols : (r + 1) * cols, :] = turned[:, :128]
        s1[r * cols : (r + 1) * cols, :] = turned[:, 128:]
    w_in = jnp.concatenate([w_in_t[...], jnp.zeros((256 - feat, hid), F32)], axis=0)
    wi_f[0], wi_f[1] = split(w_in)
    wi_b[0], wi_b[1] = split(w_in.T)
    wm_b[0], wm_b[1] = split(w_mid[...])
    wm_f[0], wm_f[1] = split(w_mid[...].T)
    out_high, out_low = split(w_out[...])
    out_high = out_high.astype(F32)
    out_low = out_low.astype(F32)
    chan = w_out.shape[0]
    stack = jnp.concatenate([out_high, out_low, jnp.zeros((128 - 2 * chan, hid), F32)], axis=0)
    wo_f[...] = stack.T.astype(BF16)
    wo_b[...] = jnp.concatenate(
        [out_high, out_low, out_high, jnp.zeros((128 - 3 * chan, hid), F32)], axis=0
    ).astype(BF16)


def forward_kernel(
    recv, s0, s1, wi, wm, wo, b_in, b_mid,
    h1_out, h2_out, r_out, cell_out, send,
    g0, g1, q, w, p, z, moments, cell_smem, sem,
):
    step = pl.program_id(0)
    peers = recv.shape[0] // 8
    blocks = peers // 8

    @pl.when(step == 0)
    def _():
        packed = jnp.concatenate([recv[pl.ds(a, peers, stride=8), :] for a in range(6)], axis=0)
        tiles = swap_groups(packed)
        for i in range(blocks):
            lanes = slice(i * LANES, (i + 1) * LANES)

            def tile(a, i=i):
                return tiles[(a * blocks + i) * 8 : (a * blocks + i) * 8 + 8]

            q[0:8, lanes] = tile(0)
            q[8:16, lanes] = tile(1)
            w[0:8, lanes] = tile(2)
            w[8:16, lanes] = tile(3)
            p[:, lanes] = tile(4)
            cell_out[i : i + 1, :] = tile(5)[0:1].astype(jnp.int32)
        copy = pltpu.make_async_copy(cell_out, cell_smem, sem)
        copy.start()
        moments[...] = jnp.zeros_like(moments)
        copy.wait()

        def gather(i, carry):
            for k in range(GROUP):
                n = i * GROUP + k
                c = cell_smem[i // 8, (i % 8) * GROUP + k]
                g0[pl.ds(n, 1), :] = s0[pl.ds(c, 1), :]
                g1[pl.ds(n, 1), :] = s1[pl.ds(c, 1), :]
            return carry

        lax.fori_loop(0, peers, gather, 0)

    start = pl.multiple_of(step * TILE, TILE)
    here = pl.ds(start, TILE)
    profile = jnp.concatenate([g0[here, :], g1[here, :]], axis=1)
    h1 = jnp.tanh(mm3(profile, wi[0], wi[1]) + b_in[...])
    h1_out[...] = h1
    h2 = jnp.tanh(mm3(h1, wm[0], wm[1]) + b_mid[...])
    h2_out[...] = h2
    high, low = split(h2)
    total = (mm(high, wo[...]) + mm(low, wo[...])).T
    zt = total[0:16] + total[16:32]
    z[:, here] = zt
    residual = w[:, here] * (zt - q[:, here])
    moments[...] += lax.dot_general(
        p[:, here], jnp.concatenate([residual] * 8, axis=0),
        (((1,), (1,)), ((), ())), precision=lax.Precision.HIGHEST, preferred_element_type=F32,
    )
    r_high, r_low = split(residual)
    r_high = r_high.astype(F32)
    r_stack = jnp.concatenate(
        [r_high, r_high, r_low.astype(F32), jnp.zeros((LANES - 48, TILE), F32)], axis=0
    )
    r_out[...] = r_stack.T.astype(BF16)

    @pl.when(step == pl.num_programs(0) - 1)
    def _():
        packed = swap_groups(to_tiles([z[0:8, :], z[8:16, :]]))
        send[pl.ds(0, peers, stride=8), :] = packed[:peers]
        send[pl.ds(1, peers, stride=8), :] = packed[peers:]
        lane_group = lax.broadcasted_iota(jnp.int32, (8, LANES), 1) // GROUP
        own = lane_group == lax.broadcasted_iota(jnp.int32, (8, LANES), 0)
        row = jnp.sum(jnp.where(own, moments[...], 0.0), axis=0, keepdims=True)
        send[pl.ds(2, peers, stride=8), :] = jnp.broadcast_to(row, (peers, LANES))


def backward_kernel(cells, h1, h2, r, wo, wm, wi, grad, i0, i1, a0, a1, c0, c1):
    step = pl.program_id(0)

    @pl.when(step == 0)
    def _():
        for acc in (a0, a1, c0, c1):
            acc[...] = jnp.zeros_like(acc)

    x2 = h2[...]
    back_mid = mm(r[...], wo[...]) * (1.0 - x2 * x2)
    x1 = h1[...]
    back_in = mm3(back_mid, wm[0], wm[1]) * (1.0 - x1 * x1)
    inc = mm3(back_in, wi[0], wi[1])
    i0[...] = inc[:, :128]
    i1[...] = inc[:, 128:]

    def scatter(i, carry):
        for k in range(0, GROUP, 2):
            n = i * GROUP + k
            g = step * (TILE // GROUP) + i
            ca = cells[g // 8, (g % 8) * GROUP + k]
            cb = cells[g // 8, (g % 8) * GROUP + k + 1]
            a0[pl.ds(ca, 1), :] += i0[pl.ds(n, 1), :]
            a1[pl.ds(ca, 1), :] += i1[pl.ds(n, 1), :]
            c0[pl.ds(cb, 1), :] += i0[pl.ds(n + 1, 1), :]
            c1[pl.ds(cb, 1), :] += i1[pl.ds(n + 1, 1), :]
        return carry

    lax.fori_loop(0, TILE // GROUP, scatter, 0)

    @pl.when(step == pl.num_programs(0) - 1)
    def _():
        rows, cols, feat = 32, 128, 200
        for row in range(rows):
            at = slice(row * cols, (row + 1) * cols)
            block = jnp.concatenate([a0[at, :] + c0[at, :], a1[at, :] + c1[at, :]], axis=1)
            grad[pl.ds(row, feat, stride=rows), :] = block.T[:feat]


def finish_kernel(recv, base, count, evolved, bias_grad):
    peers = count.shape[1]
    used = jnp.where(used_slots(count), 1.0, 0.0)
    tiles = swap_groups(
        jnp.concatenate(
            [recv[pl.ds(0, peers, stride=8), :], recv[pl.ds(1, peers, stride=8), :], used], axis=0
        )
    )
    blocks = peers // 8
    for i in range(blocks):
        lanes = slice(i * LANES, (i + 1) * LANES)
        keep = tiles[(2 * blocks + i) * 8 : (2 * blocks + i) * 8 + 8] > 0.5
        for a in range(2):
            value = tiles[(a * blocks + i) * 8 : (a * blocks + i) * 8 + 8]
            rows = slice(8 * a, 8 * a + 8)
            evolved[rows, lanes] = jnp.where(keep, value + base[rows, lanes], 0.0)
    row = jnp.sum(recv[pl.ds(2, peers, stride=8), :], axis=0, keepdims=True)
    lane = lax.broadcasted_iota(jnp.int32, (16, LANES), 1)
    chan = lax.broadcasted_iota(jnp.int32, (16, LANES), 0)
    spread = jnp.where(lane % GROUP == chan, jnp.broadcast_to(row, (16, LANES)), 0.0)
    pick = lax.broadcasted_iota(jnp.int32, (LANES, 8), 0) // GROUP == lax.broadcasted_iota(
        jnp.int32, (LANES, 8), 1
    )
    bias_grad[...] = jnp.dot(
        spread, jnp.where(pick, 1.0, 0.0), precision=lax.Precision.HIGHEST,
        preferred_element_type=F32,
    )


def shape(dims, dtype=F32):
    return jax.ShapeDtypeStruct(dims, dtype)


def exchange(data, peers):
    blocks = data.reshape(peers, 8, LANES)
    blocks = lax.all_to_all(blocks, ("gx", "gy"), split_axis=0, concat_axis=0, tiled=True)
    return blocks.reshape(peers * 8, LANES)


def per_device(
    model_state, obs_cell, obs_count, obs_value, obs_weight, predictor, bias_coef,
    weight_in, bias_in, weight_mid, bias_mid, weight_out, bias_out,
):
    feat, rows, cols = model_state.shape
    slots = obs_cell.shape[1]
    peers = obs_count.shape[1]
    hid = weight_mid.shape[0]
    cells = rows * cols
    send, base = pl.pallas_call(
        request_kernel,
        out_shape=(shape((peers * 8, LANES)), shape((16, slots))),
        name="request",
    )(obs_cell, obs_count, obs_value, obs_weight, predictor, bias_coef, bias_out[:, None])
    recv = exchange(send, peers)
    s0, s1, wi_f, wi_b, wm_f, wm_b, wo_f, wo_b = pl.pallas_call(
        prepare_kernel,
        out_shape=(
            shape((cells, 128)), shape((cells, 128)),
            shape((2, 256, hid), BF16), shape((2, hid, 256), BF16),
            shape((2, hid, hid), BF16), shape((2, hid, hid), BF16),
            shape((hid, 128), BF16), shape((128, hid), BF16),
        ),
        name="prepare",
        cost_estimate=pl.CostEstimate(flops=10**7, transcendentals=0, bytes_accessed=15 * 10**6),
    )(model_state.reshape(feat * rows, cols), weight_in.T, weight_mid, weight_out)

    def whole(dims):
        return pl.BlockSpec(dims, lambda i: (0,) * len(dims))

    steps = slots // TILE
    h1, h2, residual, cell, reply = pl.pallas_call(
        forward_kernel,
        grid=(steps,),
        in_specs=[
            whole((peers * 8, LANES)), whole((cells, 128)), whole((cells, 128)),
            whole((2, 256, hid)), whole((2, hid, hid)), whole((hid, 128)),
            whole((1, hid)), whole((1, hid)),
        ],
        out_specs=[
            pl.BlockSpec((TILE, hid), lambda i: (i, 0)),
            pl.BlockSpec((TILE, hid), lambda i: (i, 0)),
            pl.BlockSpec((TILE, 128), lambda i: (i, 0)),
            whole((slots // LANES, LANES)),
            whole((peers * 8, LANES)),
        ],
        out_shape=(
            shape((slots, hid)), shape((slots, hid)), shape((slots, 128), BF16),
            shape((slots // LANES, LANES), jnp.int32), shape((peers * 8, LANES)),
        ),
        scratch_shapes=[
            pltpu.VMEM((slots, 128), F32), pltpu.VMEM((slots, 128), F32),
            pltpu.VMEM((16, slots), F32), pltpu.VMEM((16, slots), F32),
            pltpu.VMEM((8, slots), F32), pltpu.VMEM((16, slots), F32),
            pltpu.VMEM((8, LANES), F32),
            pltpu.SMEM((slots // LANES, LANES), jnp.int32),
            pltpu.SemaphoreType.DMA(()),
        ],
        name="forward",
        cost_estimate=pl.CostEstimate(
            flops=6 * slots * hid * (256 + hid + 128), transcendentals=2 * slots * hid,
            bytes_accessed=25 * 10**6,
        ),
    )(recv, s0, s1, wi_f, wm_f, wo_f, bias_in[None, :], bias_mid[None, :])
    back = exchange(reply, peers)
    gradient = pl.pallas_call(
        backward_kernel,
        grid=(steps,),
        in_specs=[
            pl.BlockSpec(memory_space=pltpu.SMEM),
            pl.BlockSpec((TILE, hid), lambda i: (i, 0)),
            pl.BlockSpec((TILE, hid), lambda i: (i, 0)),
            pl.BlockSpec((TILE, 128), lambda i: (i, 0)),
            whole((128, hid)), whole((2, hid, hid)), whole((2, hid, 256)),
        ],
        out_specs=whole((feat * rows, cols)),
        out_shape=shape((feat * rows, cols)),
        scratch_shapes=[pltpu.VMEM((TILE, 128), F32), pltpu.VMEM((TILE, 128), F32)]
        + [pltpu.VMEM((cells, 128), F32) for _ in range(4)],
        name="backward",
        cost_estimate=pl.CostEstimate(
            flops=6 * slots * hid * (256 + hid + 128), transcendentals=0,
            bytes_accessed=25 * 10**6,
        ),
    )(cell, h1, h2, residual, wo_b, wm_b, wi_b)
    evolved, bias_gradient = pl.pallas_call(
        finish_kernel,
        out_shape=(shape((16, slots)), shape((16, 8))),
        name="finish",
    )(back, base, obs_count)
    return gradient.reshape(feat, rows, cols), evolved, bias_gradient


def solution(mesh):
    in_specs = (
        P(None, "gx", "gy"),
        P(("gx", "gy"), None),
        P(("gx", "gy"), None),
        P(None, ("gx", "gy")),
        P(None, ("gx", "gy")),
        P(None, ("gx", "gy")),
        P(),
        P(),
        P(),
        P(),
        P(),
        P(),
        P(),
    )
    out_specs = (P(None, "gx", "gy"), P(None, ("gx", "gy")), P())
    return jax.shard_map(
        per_device, mesh=mesh, in_specs=in_specs, out_specs=out_specs, check_vma=False
    )
```

time: 251 us -> 105 us (0.42); the launches traced: 248 us -> 105 us
  blocking collectives: 81.2 us -> 0 us
  Pallas kernels: 0 us -> 74.9 us
  matrix products: 63.7 us -> 0 us
  waiting for transfers between devices: 33 us -> 1.7 us
  other arithmetic: 19.9 us -> 0 us
  local copies, waits for them, and re-layouts: 25.1 us -> 8.19 us
  starting transfers between devices: 23.6 us -> 19.6 us
    psum x1 -> x0, blocking collectives: 81.2 us -> none  [per_device(): bias_gradient = lax.psum(bias_part, ('gx', 'gy'))]
    pallas_call x0 -> x5, Pallas kernels: none -> 74.9 us  [the longest x1 30.7 us: per_device(): pl.pallas_call(backward_kernel, grid=(steps,), in_specs=[pl.BlockSpec(mem...]
    dot_general x8 -> x0, matrix products: 63.7 us -> none  [product(): jnp.dot(lhs_array, rhs_array, preferred_element_type=jnp.float32, precisi...]
    all_to_all x3 -> x2, waiting for transfers between devices: 33 us -> 1.7 us  [exchange(): lax.all_to_all(blocks, ('gx', 'gy'), split_axis=0, concat_axis=0, tiled=T...]
    scatter-add x1 -> x0, other arithmetic: 14.1 us -> none  [per_device(): jnp.zeros((features, block_rows * block_cols), jnp.float32)]
    gather x1 -> x0, local copies, waits for them, and re-layouts: 10.8 us -> none  [per_device(): jnp.take(model_state.reshape(features, block_rows * block_cols), asked_ce...]
    unnamed x25 -> x6, local copies, waits for them, and re-layouts: 10.6 us -> 4.31 us
    all_to_all x3 -> x2, starting transfers between devices: 23.6 us -> 19.6 us  [exchange(): lax.all_to_all(blocks, ('gx', 'gy'), split_axis=0, concat_axis=0, tiled=T...]
  transfers between devices with their start and end apart: 3 -> 2, of which waited for: 2 -> 1; matrix products, arithmetic and copies ran while one was open for 2% -> 2% of each run, Pallas kernels for 0% -> 39%
where the time goes in v1:
time: 105 us
  Pallas kernels  74.9 us (71%)
  starting transfers between devices  19.6 us (19%)
  local copies, waits for them, and re-layouts  8.19 us (8%)
  waiting for transfers between devices  1.7 us (2%)
    pallas_call x1, Pallas kernels, per_device(): pl.pallas_call(backward_kernel, grid=(steps,), in_specs=[pl.BlockSpec(mem...  30.7 us
    pallas_call x1, Pallas kernels, per_device(): pl.pallas_call(forward_kernel, grid=(steps,), in_specs=[whole((peers * 8,...  29.6 us
    all_to_all x2, starting transfers between devices, exchange(): lax.all_to_all(blocks, ('gx', 'gy'), split_axis=0, concat_axis=0, tiled=T...  19.6 us
    pallas_call x1, Pallas kernels, per_device(): pl.pallas_call(prepare_kernel, out_shape=(shape((cells, 128)), shape((cel...  9.85 us
    unnamed x6, local copies, waits for them, and re-layouts  4.31 us
    pallas_call x1, Pallas kernels, per_device(): pl.pallas_call(request_kernel, out_shape=(shape((peers * 8, LANES)), shap...  2.59 us
    pallas_call x1, Pallas kernels, per_device(): pl.pallas_call(finish_kernel, out_shape=(shape((16, slots)), shape((16, 8...  2.16 us
  transfers between devices with their start and end apart: 2, of which 1 were waited for; matrix products, arithmetic and copies ran while one was open for 2% of the time, Pallas kernels for 39%

profile of v1, /device:TPU:1, one launch (start us, length us, event | category | flops | bytes accessed | tf_op | source)
XLA Modules:
  0.0 105.0 jit_solution(1920238467556102230)
XLA Ops:
  0.6 1.4 %copy.16.coef = f32[16,8]{1,0:T(8,128)} copy(f32[16,8]{0,1:T(8,128)} %param.19) | data formatting | bytes 1024 | tf_op args[6]
  2.0 1.3 %copy.17.bias = f32[16,1]{1,0:T(8,128)} copy(f32[16,1]{0,1:T(1,128)} %bitcast.14) | data formatting | bytes 128 | tf_op jit(solution)/shard_map/broadcast_in_dim | solution.py:267
  3.3 2.6 %request.1 = (f32[1024,128]{1,0:T(8,128)}, f32[16,2048]{1,0:T(8,128)}) custom-call(s32[1,2048]{1,0:T(1,128)} %cell.1, s32[1,128]{1,0:T(1,128)} %count.3, f32[16,2048]{1,0:T(8,128)} %obs.1, f32[16,2048]{1,0:T(8,128)} %weight.1, f32[8,2048]{1,0:T(8,128)} %pred_.1, f32[16,8]{1,0:T(8,128)} %copy.16.coef, f32[16,1]{1,0:T(8,128)} %copy.17.bias), custom_call_target="tpu_custom_call" | custom-call | tf_op jit(solution)/shard_map/request/pallas_call | solution.py:263
  5.9 11.5 %all-to-all-start = ((f32[128,8,128]{2,1,0:T(8,128)}), f32[128,8,128]{2,1,0:T(8,128)S(1)}, u32[]{:S(2)}, u32[]{:S(2)}) async-start(f32[128,8,128]{2,1,0:T(8,128)} %bitcast.13), calls=%async_computation | async-start | bytes 1048576 | tf_op jit(solution)/shard_map/all_to_all | solution.py:250
  17.4 1.3 %broadcast_in_dim.10.b_in = f32[1,768]{1,0:T(1,128)} reshape(f32[768]{0:T(1024)} %param.21) | data formatting | bytes 6144 | tf_op jit(solution)/shard_map/broadcast_in_dim | solution.py:317
  18.7 1.3 %broadcast_in_dim.11.b_mid = f32[1,768]{1,0:T(1,128)} reshape(f32[768]{0:T(1024)} %param.23) | data formatting | bytes 6144 | tf_op jit(solution)/shard_map/broadcast_in_dim | solution.py:317
  19.9 9.8 %prepare.1 = (f32[4096,128]{1,0:T(8,128)}, f32[4096,128]{1,0:T(8,128)}, bf16[2,256,768]{2,1,0:T(8,128)(2,1)}, bf16[2,768,256]{2,1,0:T(8,128)(2,1)}, bf16[2,768,7...) custom-call(f32[6400,128]{1,0:T(8,128)} %bitcast.8, ...), custom_call_target="tpu_custom_call" | custom-call | flops 10000000 | bytes 15000000 | tf_op jit(solution)/shard_map/prepare/pallas_call | solution.py:269
  29.8 1.7 %all-to-all-done = f32[128,8,128]{2,1,0:T(8,128)S(1)} async-done(((f32[128,8,128]{2,1,0:T(8,128)}), f32[128,8,128]{2,1,0:T(8,128)S(1)}, u32[]{:S(2)}, u32[]{:S(2)}) %all-to-all-start) | async-done | bytes 524320 | tf_op jit(solution)/shard_map/all_to_all | solution.py:250
  31.5 0.0 copy-start.1
  31.5 0.8 copy-done.1
  32.3 29.6 %forward.1 = (f32[2048,768]{1,0:T(8,128)}, f32[2048,768]{1,0:T(8,128)}, bf16[2048,128]{1,0:T(8,128)(2,1)}, s32[16,128]{1,0:T(8,128)}, f32[1024,128]{1,0:T(8,128)}) custom-call(f32[1024,128]{1,0:T(8,128)} %bitcast.11, f32[4096,128]{1,0:T(8,128)} %get-tuple-element.21.s0, f32[4096,128]{1,0:T(8,128)} %get-tuple-element.22.s1, ...), custom_call_target="tpu_custom_call" | custom-call | flops 10871635968 | bytes 25000000 | tf_op jit(solution)/shard_map/forward/pallas_call | solution.py:285
  61.9 8.1 %all-to-all-start.1 = ((f32[128,8,128]{2,1,0:T(8,128)}), f32[128,8,128]{2,1,0:T(8,128)S(1)}, u32[]{:S(2)}, u32[]{:S(2)}) async-start(f32[128,8,128]{2,1,0:T(8,128)} %bitcast.12), calls=%async_computation.1 | async-start | bytes 1048576 | tf_op jit(solution)/shard_map/all_to_all | solution.py:250
  70.0 30.7 %backward.1 = f32[6400,128]{1,0:T(8,128)} custom-call(s32[16,128]{1,0:T(8,128)} %get-tuple-element.26.cells, f32[2048,768]{1,0:T(8,128)} %get-tuple-element.27.h1, f32[2048,768]{1,0:T(8,128)} %get-tuple-element.28.h2, bf16[2048,128]{1,0:T(8,128)(2,1)} %get-tuple-element.29.r, bf16[128,768]{1,0:T(8,128)(2,1)} %get-tuple-element.30.wo, ...), custom_call_target="tpu_custom_call" | custom-call | flops 10871635968 | bytes 25000000 | tf_op jit(solution)/shard_map/backward/pallas_call | solution.py:319
  100.7 0.0 all-to-all-done.1
  100.7 0.0 copy-start
  100.7 0.8 copy-done
  101.5 2.2 %finish.1 = (f32[16,2048]{1,0:T(8,128)}, f32[16,8]{1,0:T(8,128)}) custom-call(f32[1024,128]{1,0:T(8,128)} %bitcast.9, f32[16,2048]{1,0:T(8,128)} %get-tuple-element.34.base, s32[1,128]{1,0:T(1,128)} %count.3), custom_call_target="tpu_custom_call" | custom-call | tf_op jit(solution)/shard_map/finish/pallas_call | solution.py:339
  103.7 1.4 %copy.18 = f32[16,8]{0,1:T(8,128)} copy(f32[16,8]{1,0:T(8,128)} %get-tuple-element.39) | data formatting | bytes 1024
Async XLA Ops:
  5.9 25.6 %all-to-all-start = ((f32[128,8,128]{2,1,0:T(8,128)}), f32[128,8,128]{2,1,0:T(8,128)S(1)}, u32[]{:S(2)}, u32[]{:S(2)}) async-start(f32[128,8,128]{2,1,0:T(8,128)} %bitcast.13), calls=%async_computation | async-start | bytes 1048576 | tf_op jit(solution)/shard_map/all_to_all | solution.py:250
  31.5 0.8 copy-start.1
  61.9 38.8 %all-to-all-start.1 = ((f32[128,8,128]{2,1,0:T(8,128)}), f32[128,8,128]{2,1,0:T(8,128)S(1)}, u32[]{:S(2)}, u32[]{:S(2)}) async-start(f32[128,8,128]{2,1,0:T(8,128)} %bitcast.12), calls=%async_computation.1 | async-start | bytes 1048576 | tf_op jit(solution)/shard_map/all_to_all | solution.py:250
  100.7 0.8 copy-start

commit v2 on v1

--- a/solution.py
+++ b/solution.py
@@ -1,5 +1,3 @@
-import functools
-
 import jax
 import jax.numpy as jnp
 from jax import lax
@@ -23,9 +21,15 @@
     return jnp.dot(lhs, rhs, preferred_element_type=F32)
 
 
+def mm3_of(high, low, rhs_high, rhs_low):
+    return mm(
+        jnp.concatenate([high, low, high], axis=1),
+        jnp.concatenate([rhs_high, rhs_high, rhs_low], axis=0),
+    )
+
+
 def mm3(lhs, rhs_high, rhs_low):
-    high, low = split(lhs)
-    return mm(high, rhs_high) + (mm(low, rhs_high) + mm(high, rhs_low))
+    return mm3_of(*split(lhs), rhs_high, rhs_low)
 
 
 def swap_groups(x):
@@ -55,10 +59,12 @@
     return slot.astype(F32) < counts
 
 
-def request_kernel(cell, count, obs, weight, pred, coef, bias, send, base):
+def request_kernel(cell, count, obs, weight, pred, coef_t, bias, send, base):
     peers = count.shape[1]
-    linear = jnp.broadcast_to(bias[...], obs.shape)
-    for i in range(pred.shape[0]):
+    coef = jnp.concatenate([coef_t[...], jnp.broadcast_to(bias[...], coef_t.shape)], axis=0).T
+    preds = pred.shape[0]
+    linear = jnp.broadcast_to(coef[:, preds : preds + 1], obs.shape)
+    for i in range(preds):
         linear = linear + coef[:, i : i + 1] * pred[i : i + 1, :]
     base[...] = linear
     target = obs[...] - linear
@@ -100,51 +106,70 @@
 
 
 def forward_kernel(
-    recv, s0, s1, wi, wm, wo, b_in, b_mid,
+    recv, s0_hbm, s1_hbm, wi_hbm, wm_hbm, wo_hbm, b_in, b_mid,
     h1_out, h2_out, r_out, cell_out, send,
-    g0, g1, q, w, p, z, moments, cell_smem, sem,
+    s0, s1, wi, wm, wo, g0, g1, q, w, p, z, moments, cell_smem, sems,
 ):
     step = pl.program_id(0)
     peers = recv.shape[0] // 8
     blocks = peers // 8
 
+    def fetch(row, to_row):
+        g0[pl.ds(to_row, 1), :] = s0[pl.ds(row, 1), :]
+        g1[pl.ds(to_row, 1), :] = s1[pl.ds(row, 1), :]
+
     @pl.when(step == 0)
     def _():
+        copies = [
+            pltpu.make_async_copy(source, target, sems.at[i])
+            for i, (source, target) in enumerate(
+                ((s0_hbm, s0), (s1_hbm, s1), (wi_hbm, wi), (wm_hbm, wm), (wo_hbm, wo))
+            )
+        ]
+        for copy in copies:
+            copy.start()
         packed = jnp.concatenate([recv[pl.ds(a, peers, stride=8), :] for a in range(6)], axis=0)
         tiles = swap_groups(packed)
+
+        def tile(a, i):
+            return tiles[(a * blocks + i) * 8 : (a * blocks + i) * 8 + 8]
+
+        for i in range(blocks):
+            cell_out[i : i + 1, :] = tile(5, i)[0:1].astype(jnp.int32)
+        copy = pltpu.make_async_copy(cell_out, cell_smem, sems.at[5])
+        copy.start()
         for i in range(blocks):
             lanes = slice(i * LANES, (i + 1) * LANES)
-
-            def tile(a, i=i):
-                return tiles[(a * blocks + i) * 8 : (a * blocks + i) * 8 + 8]
-
-            q[0:8, lanes] = tile(0)
-            q[8:16, lanes] = tile(1)
-            w[0:8, lanes] = tile(2)
-            w[8:16, lanes] = tile(3)
-            p[:, lanes] = tile(4)
-            cell_out[i : i + 1, :] = tile(5)[0:1].astype(jnp.int32)
-        copy = pltpu.make_async_copy(cell_out, cell_smem, sem)
-        copy.start()
+            q[0:8, lanes] = tile(0, i)
+            q[8:16, lanes] = tile(1, i)
+            w[0:8, lanes] = tile(2, i)
+            w[8:16, lanes] = tile(3, i)
+            p[:, lanes] = tile(4, i)
         moments[...] = jnp.zeros_like(moments)
         copy.wait()
+        copies[0].wait()
+        copies[1].wait()
 
         def gather(i, carry):
             for k in range(GROUP):
-                n = i * GROUP + k
-                c = cell_smem[i // 8, (i % 8) * GROUP + k]
-                g0[pl.ds(n, 1), :] = s0[pl.ds(c, 1), :]
-                g1[pl.ds(n, 1), :] = s1[pl.ds(c, 1), :]
+                fetch(cell_smem[i // 8, (i % 8) * GROUP + k], i * GROUP + k)
             return carry
 
-        lax.fori_loop(0, peers, gather, 0)
+        lax.fori_loop(0, TILE // GROUP, gather, 0)
+        for copy in copies[2:]:
+            copy.wait()
 
     start = pl.multiple_of(step * TILE, TILE)
     here = pl.ds(start, TILE)
-    profile = jnp.concatenate([g0[here, :], g1[here, :]], axis=1)
-    h1 = jnp.tanh(mm3(profile, wi[0], wi[1]) + b_in[...])
+    high, low = split(jnp.concatenate([g0[here, :], g1[here, :]], axis=1))
+    following = jnp.minimum(step + 1, pl.num_programs(0) - 1)
+    for n in range(TILE):
+        fetch(
+            cell_smem[following * (TILE // LANES) + n // LANES, n % LANES], following * TILE + n
+        )
+    h1 = jnp.tanh(mm3_of(high, low, wi[0], wi[1]) + b_in[...][None, :])
     h1_out[...] = h1
-    h2 = jnp.tanh(mm3(h1, wm[0], wm[1]) + b_mid[...])
+    h2 = jnp.tanh(mm3(h1, wm[0], wm[1]) + b_mid[...][None, :])
     h2_out[...] = h2
     high, low = split(h2)
     total = (mm(high, wo[...]) + mm(low, wo[...])).T
@@ -173,43 +198,85 @@
         send[pl.ds(2, peers, stride=8), :] = jnp.broadcast_to(row, (peers, LANES))
 
 
-def backward_kernel(cells, h1, h2, r, wo, wm, wi, grad, i0, i1, a0, a1, c0, c1):
+def backward_kernel(
+    cells, h1_hbm, h2_hbm, r, wo_hbm, wm_hbm, wi_hbm, grad,
+    h1, h2, wo, wm, wi, i0, i1, a0, a1, c0, c1, out, sems, h1_sems, h2_sems, out_sems,
+):
     step = pl.program_id(0)
+    last = pl.num_programs(0) - 1
+    steps = h1.shape[0] // TILE
+
+    def tile_copy(source, target, some_sems, i):
+        rows = pl.ds(pl.multiple_of(i * TILE, TILE), TILE)
+        return pltpu.make_async_copy(source.at[rows, :], target.at[rows, :], some_sems.at[i])
 
     @pl.when(step == 0)
     def _():
-        for acc in (a0, a1, c0, c1):
+        weights = [
+            pltpu.make_async_copy(source, target, sems.at[i])
+            for i, (source, target) in enumerate(((wo_hbm, wo), (wm_hbm, wm), (wi_hbm, wi)))
+        ]
+        weights[0].start()
+        tile_copy(h2_hbm, h2, h2_sems, 0).start()
+        weights[1].start()
+        tile_copy(h1_hbm, h1, h1_sems, 0).start()
+        weights[2].start()
+        for i in range(1, steps):
+            tile_copy(h2_hbm, h2, h2_sems, i).start()
+            tile_copy(h1_hbm, h1, h1_sems, i).start()
+        for acc in (a0, a1, c0, c1, i0, i1):
             acc[...] = jnp.zeros_like(acc)
-
-    x2 = h2[...]
-    back_mid = mm(r[...], wo[...]) * (1.0 - x2 * x2)
-    x1 = h1[...]
-    back_in = mm3(back_mid, wm[0], wm[1]) * (1.0 - x1 * x1)
-    inc = mm3(back_in, wi[0], wi[1])
-    i0[...] = inc[:, :128]
-    i1[...] = inc[:, 128:]
-
-    def scatter(i, carry):
-        for k in range(0, GROUP, 2):
-            n = i * GROUP + k
-            g = step * (TILE // GROUP) + i
-            ca = cells[g // 8, (g % 8) * GROUP + k]
-            cb = cells[g // 8, (g % 8) * GROUP + k + 1]
-            a0[pl.ds(ca, 1), :] += i0[pl.ds(n, 1), :]
-            a1[pl.ds(ca, 1), :] += i1[pl.ds(n, 1), :]
-            c0[pl.ds(cb, 1), :] += i0[pl.ds(n + 1, 1), :]
-            c1[pl.ds(cb, 1), :] += i1[pl.ds(n + 1, 1), :]
-        return carry
-
-    lax.fori_loop(0, TILE // GROUP, scatter, 0)
-
-    @pl.when(step == pl.num_programs(0) - 1)
+        for copy in weights:
+            copy.wait()
+
+    tile_copy(h2_hbm, h2, h2_sems, step).wait()
+    tile_copy(h1_hbm, h1, h1_sems, step).wait()
+    start = pl.multiple_of(step * TILE, TILE)
+
+    def add(first, second, n):
+        a0[pl.ds(first, 1), :] += i0[pl.ds(n, 1), :]
+        a1[pl.ds(first, 1), :] += i1[pl.ds(n, 1), :]
+        c0[pl.ds(second, 1), :] += i0[pl.ds(n + 1, 1), :]
+        c1[pl.ds(second, 1), :] += i1[pl.ds(n + 1, 1), :]
+
+    before = jnp.maximum(step - 1, 0) * (TILE // LANES)
+    for n in range(0, TILE, 2):
+        row = before + n // LANES
+        add(cells[row, n % LANES], cells[row, n % LANES + 1], n)
+    halves = [slice(0, TILE // 2), slice(TILE // 2, TILE)]
+    mids = []
+    for s in halves:
+        x2 = h2[pl.ds(start + s.start, TILE // 2), :]
+        mids.append(mm(r[s, :], wo[...]) * (1.0 - x2 * x2))
+    ins = []
+    for s, back_mid in zip(halves, mids):
+        x1 = h1[pl.ds(start + s.start, TILE // 2), :]
+        ins.append(mm3(back_mid, wm[0], wm[1]) * (1.0 - x1 * x1))
+    for s, back_in in zip(halves, ins):
+        increment = mm3(back_in, wi[0], wi[1])
+        i0[s, :] = increment[:, :128]
+        i1[s, :] = increment[:, 128:]
+
+    @pl.when(step == last)
     def _():
-        rows, cols, feat = 32, 128, 200
+        def scatter(i, carry):
+            row = last * (TILE // LANES) + i // 8
+            for k in range(0, GROUP, 2):
+                at = (i % 8) * GROUP + k
+                add(cells[row, at], cells[row, at + 1], i * GROUP + k)
+            return carry
+
+        lax.fori_loop(0, TILE // GROUP, scatter, 0)
+        feat, rows, cols = grad.shape
+        copies = []
         for row in range(rows):
             at = slice(row * cols, (row + 1) * cols)
             block = jnp.concatenate([a0[at, :] + c0[at, :], a1[at, :] + c1[at, :]], axis=1)
-            grad[pl.ds(row, feat, stride=rows), :] = block.T[:feat]
+            out[row] = block.T[:feat]
+            copies.append(pltpu.make_async_copy(out.at[row], grad.at[:, row, :], out_sems.at[row]))
+            copies[-1].start()
+        for copy in copies:
+            copy.wait()
 
 
 def finish_kernel(recv, base, count, evolved, bias_grad):
@@ -229,11 +296,13 @@
             rows = slice(8 * a, 8 * a + 8)
             evolved[rows, lanes] = jnp.where(keep, value + base[rows, lanes], 0.0)
     row = jnp.sum(recv[pl.ds(2, peers, stride=8), :], axis=0, keepdims=True)
-    lane = lax.broadcasted_iota(jnp.int32, (16, LANES), 1)
-    chan = lax.broadcasted_iota(jnp.int32, (16, LANES), 0)
-    spread = jnp.where(lane % GROUP == chan, jnp.broadcast_to(row, (16, LANES)), 0.0)
-    pick = lax.broadcasted_iota(jnp.int32, (LANES, 8), 0) // GROUP == lax.broadcasted_iota(
-        jnp.int32, (LANES, 8), 1
+    lane = lax.broadcasted_iota(jnp.int32, (8, LANES), 1)
+    spread = jnp.where(
+        lane // GROUP == lax.broadcasted_iota(jnp.int32, (8, LANES), 0),
+        jnp.broadcast_to(row, (8, LANES)), 0.0,
+    )
+    pick = lax.broadcasted_iota(jnp.int32, (LANES, 16), 0) % GROUP == lax.broadcasted_iota(
+        jnp.int32, (LANES, 16), 1
     )
     bias_grad[...] = jnp.dot(
         spread, jnp.where(pick, 1.0, 0.0), precision=lax.Precision.HIGHEST,
@@ -241,8 +310,16 @@
     )
 
 
+def limit(mebibytes):
+    return pltpu.CompilerParams(vmem_limit_bytes=mebibytes * 2**20)
+
+
+def stay(x):
+    return pltpu.with_memory_space_constraint(x, pltpu.HBM)
+
+
 def shape(dims, dtype=F32):
-    return jax.ShapeDtypeStruct(dims, dtype)
+    return pltpu.HBM(dims, dtype)
 
 
 def exchange(data, peers):
@@ -264,7 +341,7 @@
         request_kernel,
         out_shape=(shape((peers * 8, LANES)), shape((16, slots))),
         name="request",
-    )(obs_cell, obs_count, obs_value, obs_weight, predictor, bias_coef, bias_out[:, None])
+    )(obs_cell, obs_count, obs_value, obs_weight, predictor, bias_coef.T, bias_out[None, :])
     recv = exchange(send, peers)
     s0, s1, wi_f, wi_b, wm_f, wm_b, wo_f, wo_b = pl.pallas_call(
         prepare_kernel,
@@ -282,13 +359,13 @@
         return pl.BlockSpec(dims, lambda i: (0,) * len(dims))
 
     steps = slots // TILE
+    in_hbm = pl.BlockSpec(memory_space=pltpu.HBM)
     h1, h2, residual, cell, reply = pl.pallas_call(
         forward_kernel,
         grid=(steps,),
         in_specs=[
-            whole((peers * 8, LANES)), whole((cells, 128)), whole((cells, 128)),
-            whole((2, 256, hid)), whole((2, hid, hid)), whole((hid, 128)),
-            whole((1, hid)), whole((1, hid)),
+            whole((peers * 8, LANES)), in_hbm, in_hbm, in_hbm, in_hbm, in_hbm,
+            whole((hid,)), whole((hid,)),
         ],
         out_specs=[
             pl.BlockSpec((TILE, hid), lambda i: (i, 0)),
@@ -302,34 +379,47 @@
             shape((slots // LANES, LANES), jnp.int32), shape((peers * 8, LANES)),
         ),
         scratch_shapes=[
+            pltpu.VMEM((cells, 128), F32), pltpu.VMEM((cells, 128), F32),
+            pltpu.VMEM((2, 256, hid), BF16), pltpu.VMEM((2, hid, hid), BF16),
+            pltpu.VMEM((hid, 128), BF16),
             pltpu.VMEM((slots, 128), F32), pltpu.VMEM((slots, 128), F32),
             pltpu.VMEM((16, slots), F32), pltpu.VMEM((16, slots), F32),
             pltpu.VMEM((8, slots), F32), pltpu.VMEM((16, slots), F32),
             pltpu.VMEM((8, LANES), F32),
             pltpu.SMEM((slots // LANES, LANES), jnp.int32),
-            pltpu.SemaphoreType.DMA(()),
+            pltpu.SemaphoreType.DMA((6,)),
         ],
         name="forward",
+        compiler_params=limit(48),
         cost_estimate=pl.CostEstimate(
             flops=6 * slots * hid * (256 + hid + 128), transcendentals=2 * slots * hid,
             bytes_accessed=25 * 10**6,
         ),
-    )(recv, s0, s1, wi_f, wm_f, wo_f, bias_in[None, :], bias_mid[None, :])
+    )(recv, *map(stay, (s0, s1, wi_f, wm_f, wo_f)), bias_in, bias_mid)
     back = exchange(reply, peers)
     gradient = pl.pallas_call(
         backward_kernel,
         grid=(steps,),
         in_specs=[
             pl.BlockSpec(memory_space=pltpu.SMEM),
-            pl.BlockSpec((TILE, hid), lambda i: (i, 0)),
-            pl.BlockSpec((TILE, hid), lambda i: (i, 0)),
+            in_hbm, in_hbm,
             pl.BlockSpec((TILE, 128), lambda i: (i, 0)),
-            whole((128, hid)), whole((2, hid, hid)), whole((2, hid, 256)),
+            in_hbm, in_hbm, in_hbm,
         ],
-        out_specs=whole((feat * rows, cols)),
-        out_shape=shape((feat * rows, cols)),
-        scratch_shapes=[pltpu.VMEM((TILE, 128), F32), pltpu.VMEM((TILE, 128), F32)]
-        + [pltpu.VMEM((cells, 128), F32) for _ in range(4)],
+        out_specs=in_hbm,
+        out_shape=shape((feat, rows, cols)),
+        scratch_shapes=[
+            pltpu.VMEM((slots, hid), F32), pltpu.VMEM((slots, hid), F32),
+            pltpu.VMEM((128, hid), BF16), pltpu.VMEM((2, hid, hid), BF16),
+            pltpu.VMEM((2, hid, 256), BF16),
+            pltpu.VMEM((TILE, 128), F32), pltpu.VMEM((TILE, 128), F32),
+        ]
+        + [pltpu.VMEM((cells, 128), F32) for _ in range(4)]
+        + [
+            pltpu.VMEM((rows, feat, cols), F32),
+            pltpu.SemaphoreType.DMA((3,)), pltpu.SemaphoreType.DMA((steps,)),
+            pltpu.SemaphoreType.DMA((steps,)), pltpu.SemaphoreType.DMA((rows,)),
+        ],
         name="backward",
         cost_estimate=pl.CostEstimate(
             flops=6 * slots * hid * (256 + hid + 128), transcendentals=0,
@@ -338,10 +428,11 @@
     )(cell, h1, h2, residual, wo_b, wm_b, wi_b)
     evolved, bias_gradient = pl.pallas_call(
         finish_kernel,
-        out_shape=(shape((16, slots)), shape((16, 8))),
+        out_shape=(shape((16, slots)), shape((8, 16))),
         name="finish",
+        compiler_params=limit(8),
     )(back, base, obs_count)
-    return gradient.reshape(feat, rows, cols), evolved, bias_gradient
+    return gradient, evolved, bias_gradient.T
 
 
 def solution(mesh):

time: 105 us -> 81.8 us (0.78)
  Pallas kernels: 74.9 us -> 59.5 us
  local copies, waits for them, and re-layouts: 8.19 us -> 0.03 us
  waiting for transfers between devices: 1.7 us -> 4.21 us
  starting transfers between devices: 19.6 us -> 17.1 us
    pallas_call x1, Pallas kernels: 30.7 us -> 22.3 us  [per_device(): pl.pallas_call(backward_kernel, grid=(steps,), in_specs=[pl.BlockSpec(mem...]
    pallas_call x1, Pallas kernels: 29.6 us -> 23.6 us  [per_device(): pl.pallas_call(forward_kernel, grid=(steps,), in_specs=[whole((peers * 8,...]
    unnamed x6 -> x8, local copies, waits for them, and re-layouts: 4.31 us -> 0.03 us
    broadcast_in_dim x3 -> x0, local copies, waits for them, and re-layouts: 3.88 us -> none  [the longest x1 1.33 us: per_device(): bias_out[:, None]]
    all_to_all x2, waiting for transfers between devices: 1.7 us -> 4.21 us  [exchange(): lax.all_to_all(blocks, ('gx', 'gy'), split_axis=0, concat_axis=0, tiled=T...]
    all_to_all x2, starting transfers between devices: 19.6 us -> 17.1 us  [exchange(): lax.all_to_all(blocks, ('gx', 'gy'), split_axis=0, concat_axis=0, tiled=T...]
    pallas_call x1, Pallas kernels: 2.16 us -> 1.06 us  [per_device(): pl.pallas_call(finish_kernel, out_shape=(shape((16, slots)), shape((8, 16...]
  transfers between devices with their start and end apart: 2 -> 2, of which waited for: 1 -> 1; matrix products, arithmetic and copies ran while one was open for 2% -> 0% of each run, Pallas kernels for 39% -> 39%
where the time goes in v2:
time: 81.8 us; the launch traced here: 81.5 us
  Pallas kernels  59.5 us (73%)
  starting transfers between devices  17.1 us (21%)
  waiting for transfers between devices  4.21 us (5%)
    pallas_call x1, Pallas kernels, per_device(): pl.pallas_call(forward_kernel, grid=(steps,), in_specs=[whole((peers * 8,...  23.6 us
    pallas_call x1, Pallas kernels, per_device(): pl.pallas_call(backward_kernel, grid=(steps,), in_specs=[pl.BlockSpec(mem...  22.3 us
    all_to_all x2, starting transfers between devices, exchange(): lax.all_to_all(blocks, ('gx', 'gy'), split_axis=0, concat_axis=0, tiled=T...  17.1 us
    pallas_call x1, Pallas kernels, per_device(): pl.pallas_call(prepare_kernel, out_shape=(shape((cells, 128)), shape((cel...  9.86 us
    all_to_all x2, waiting for transfers between devices, exchange(): lax.all_to_all(blocks, ('gx', 'gy'), split_axis=0, concat_axis=0, tiled=T...  4.21 us
    pallas_call x1, Pallas kernels, per_device(): pl.pallas_call(request_kernel, out_shape=(shape((peers * 8, LANES)), shap...  2.63 us
  transfers between devices with their start and end apart: 2, of which 1 were waited for; matrix products, arithmetic and copies ran while one was open for 0% of the time, Pallas kernels for 39%

profile of v2, /device:TPU:1, one launch (start us, length us, event | category | flops | bytes accessed | tf_op | source)
XLA Modules:
  0.0 81.5 jit_solution(2438859155634679955)
XLA Ops:
  0.6 2.6 %request.1 = (f32[1024,128]{1,0:T(8,128)}, f32[16,2048]{1,0:T(8,128)}) custom-call(s32[1,2048]{1,0:T(1,128)} %cell.1, s32[1,128]{1,0:T(1,128)} %count.3, f32[16,2048]{1,0:T(8,128)} %obs.1, f32[16,2048]{1,0:T(8,128)} %weight.1, f32[8,2048]{1,0:T(8,128)} %pred_.1, f32[8,16]{1,0:T(8,128)} %bitcast.15, f32[1,16]{1,0:T(1,128)} %bitcast.16), custom_call_target="tpu_custom_call" | custom-call | tf_op jit(solution)/shard_map/request/pallas_call | solution.py:340
  3.3 11.5 %all-to-all-start = ((f32[128,8,128]{2,1,0:T(8,128)}), f32[128,8,128]{2,1,0:T(8,128)S(1)}, u32[]{:S(2)}, u32[]{:S(2)}) async-start(f32[128,8,128]{2,1,0:T(8,128)} %bitcast.14), calls=%async_computation | async-start | bytes 1048576 | tf_op jit(solution)/shard_map/all_to_all | solution.py:327
  14.8 0.0 copy-start.2
  14.8 0.0 copy-start.3
  14.8 9.9 %prepare.1 = (f32[4096,128]{1,0:T(8,128)}, f32[4096,128]{1,0:T(8,128)}, bf16[2,256,768]{2,1,0:T(8,128)(2,1)}, bf16[2,768,256]{2,1,0:T(8,128)(2,1)}, bf16[2,768,7...) custom-call(f32[6400,128]{1,0:T(8,128)} %bitcast.11, ...), custom_call_target="tpu_custom_call" | custom-call | flops 10000000 | bytes 15000000 | tf_op jit(solution)/shard_map/prepare/pallas_call | solution.py:346
  24.6 4.2 %all-to-all-done = f32[128,8,128]{2,1,0:T(8,128)S(1)} async-done(((f32[128,8,128]{2,1,0:T(8,128)}), f32[128,8,128]{2,1,0:T(8,128)S(1)}, u32[]{:S(2)}, u32[]{:S(2)}) %all-to-all-start) | async-done | bytes 524320 | tf_op jit(solution)/shard_map/all_to_all | solution.py:327
  28.9 0.0 copy-done.2
  28.9 0.0 copy-done.3
  28.9 23.6 %forward.1 = (f32[2048,768]{1,0:T(8,128)}, f32[2048,768]{1,0:T(8,128)}, bf16[2048,128]{1,0:T(8,128)(2,1)}, s32[16,128]{1,0:T(8,128)}, f32[1024,128]{1,0:T(8,128)}) custom-call(f32[1024,128]{1,0:T(8,128)S(1)} %bitcast.10, f32[4096,128]{1,0:T(8,128)} %get-tuple-element.21.s0_hbm, f32[4096,128]{1,0:T(8,128)} %get-tuple-element.22.s1_hbm, ...), custom_call_target="tpu_custom_call" | custom-call | flops 10871635968 | bytes 25000000 | tf_op jit(solution)/shard_map/forward/pallas_call | solution.py:363
  52.5 5.6 %all-to-all-start.1 = ((f32[128,8,128]{2,1,0:T(8,128)}), f32[128,8,128]{2,1,0:T(8,128)S(1)}, u32[]{:S(2)}, u32[]{:S(2)}) async-start(f32[128,8,128]{2,1,0:T(8,128)} %bitcast.13), calls=%async_computation.1 | async-start | bytes 1048576 | tf_op jit(solution)/shard_map/all_to_all | solution.py:327
  58.1 0.0 copy-start
  58.1 0.0 copy-start.1
  58.1 22.3 %backward.1 = f32[200,32,128]{2,1,0:T(8,128)} custom-call(s32[16,128]{1,0:T(8,128)} %get-tuple-element.26.cells, f32[2048,768]{1,0:T(8,128)} %get-tuple-element.27.h1_hbm, f32[2048,768]{1,0:T(8,128)} %get-tuple-element.28.h2_hbm, bf16[2048,128]{1,0:T(8,128)(2,1)} %get-tuple-element.29.r, bf16[128,768]{1,0:T(8,128)(2,1)} %get-tuple-element.30.wo_hbm, ...), custom_call_target="tpu_custom_call" | custom-call | flops 10871635968 | bytes 25000000 | tf_op jit(solution)/shard_map/backward/pallas_call | solution.py:400
  80.5 0.0 all-to-all-done.1
  80.5 0.0 copy-done
  80.5 0.0 copy-done.1
  80.5 1.1 %finish.1 = (f32[16,2048]{1,0:T(8,128)}, f32[8,16]{1,0:T(8,128)}) custom-call(f32[1024,128]{1,0:T(8,128)S(1)} %bitcast.9, f32[16,2048]{1,0:T(8,128)S(1)} %copy-done, s32[1,128]{1,0:T(1,128)S(1)} %copy-done.1), custom_call_target="tpu_custom_call" | custom-call | tf_op jit(solution)/shard_map/finish/pallas_call | solution.py:429
Async XLA Ops:
  3.3 25.6 %all-to-all-start = ((f32[128,8,128]{2,1,0:T(8,128)}), f32[128,8,128]{2,1,0:T(8,128)S(1)}, u32[]{:S(2)}, u32[]{:S(2)}) async-start(f32[128,8,128]{2,1,0:T(8,128)} %bitcast.14), calls=%async_computation | async-start | bytes 1048576 | tf_op jit(solution)/shard_map/all_to_all | solution.py:327
  14.8 14.1 %copy-start.2 = (f32[768]{0:T(1024)S(1)}, f32[768]{0:T(1024)}, u32[]{:S(2)}) copy-start(f32[768]{0:T(1024)} %b_in.1) | copy-start | bytes 9220
  14.8 14.1 %copy-start.3 = (f32[768]{0:T(1024)S(1)}, f32[768]{0:T(1024)}, u32[]{:S(2)}) copy-start(f32[768]{0:T(1024)} %b_mid.1) | copy-start | bytes 9220
  52.5 28.0 %all-to-all-start.1 = ((f32[128,8,128]{2,1,0:T(8,128)}), f32[128,8,128]{2,1,0:T(8,128)S(1)}, u32[]{:S(2)}, u32[]{:S(2)}) async-start(f32[128,8,128]{2,1,0:T(8,128)} %bitcast.13), calls=%async_computation.1 | async-start | bytes 1048576 | tf_op jit(solution)/shard_map/all_to_all | solution.py:327
  58.1 22.4 %copy-start = (f32[16,2048]{1,0:T(8,128)S(1)}, f32[16,2048]{1,0:T(8,128)}, u32[]{:S(2)}) copy-start(f32[16,2048]{1,0:T(8,128)} %get-tuple-element.34.base) | copy-start | bytes 393220
  58.1 22.4 %copy-start.1 = (s32[1,128]{1,0:T(1,128)S(1)}, s32[1,128]{1,0:T(1,128)}, u32[]{:S(2)}) copy-start(s32[1,128]{1,0:T(1,128)} %count.3) | copy-start | bytes 1540

commit v3 on v2

--- a/solution.py
+++ b/solution.py
@@ -10,6 +10,8 @@
 LANES = 128
 GROUP = 16
 TILE = 512
+ASK = 6
+REPLY = 3
 
 
 def split(x):
@@ -21,15 +23,22 @@
     return jnp.dot(lhs, rhs, preferred_element_type=F32)
 
 
-def mm3_of(high, low, rhs_high, rhs_low):
+def mm3(parts, rhs):
+    high, low = parts
     return mm(
         jnp.concatenate([high, low, high], axis=1),
-        jnp.concatenate([rhs_high, rhs_high, rhs_low], axis=0),
-    )
-
-
-def mm3(lhs, rhs_high, rhs_low):
-    return mm3_of(*split(lhs), rhs_high, rhs_low)
+        jnp.concatenate([rhs[0], rhs[0], rhs[1]], axis=0),
+    )
+
+
+def mm3_turned(parts, rhs):
+    high, low = parts
+    return lax.dot_general(
+        jnp.concatenate([high, low, high], axis=1),
+        jnp.concatenate([rhs[0], rhs[0], rhs[1]], axis=1),
+        (((1,), (1,)), ((), ())),
+        preferred_element_type=F32,
+    )
 
 
 def swap_groups(x):
@@ -77,58 +86,83 @@
         rows = packed[a * peers : (a + 1) * peers]
         if a in (2, 3):
             rows = jnp.where(used, rows, 0.0)
-        send[pl.ds(a, peers, stride=8), :] = rows
-
-
-def prepare_kernel(state, w_in_t, w_mid, w_out, s0, s1, wi_f, wi_b, wm_f, wm_b, wo_f, wo_b):
-    feat, rows, cols = 200, 32, 128
+        send[pl.ds(a, peers, stride=ASK), :] = rows
+
+
+def prepare_kernel(
+    state, w_in_t, w_mid_hbm, w_out, s_out, wi, wm, wo_f, wo_b,
+    columns, turned, w_mid, wi_v, wm_v, sems, in_sems, out_sems,
+):
+    feat, rows, cols = state.shape
     hid = w_mid.shape[0]
-    fill = jnp.zeros((256 - feat, cols), F32)
+    chan = w_out.shape[0]
+    loads = [
+        pltpu.make_async_copy(state.at[:, r, :], columns.at[r, :feat, :], in_sems.at[r])
+        for r in range(rows)
+    ]
+    load_mid = pltpu.make_async_copy(w_mid_hbm, w_mid, sems.at[0])
+    for copy in loads[: rows // 2]:
+        copy.start()
+    load_mid.start()
+    for copy in loads[rows // 2 :]:
+        copy.start()
     for r in range(rows):
-        block = jnp.concatenate([state[pl.ds(r, feat, stride=rows), :], fill], axis=0)
-        turned = block.T
-        s0[r * cols : (r + 1) * cols, :] = turned[:, :128]
-        s1[r * cols : (r + 1) * cols, :] = turned[:, 128:]
+        columns[r, feat:, :] = jnp.zeros((columns.shape[1] - feat, cols), F32)
     w_in = jnp.concatenate([w_in_t[...], jnp.zeros((256 - feat, hid), F32)], axis=0)
-    wi_f[0], wi_f[1] = split(w_in)
-    wi_b[0], wi_b[1] = split(w_in.T)
-    wm_b[0], wm_b[1] = split(w_mid[...])
-    wm_f[0], wm_f[1] = split(w_mid[...].T)
+    wi_v[0], wi_v[1] = split(w_in)
+    stores = [pltpu.make_async_copy(wi_v, wi, sems.at[1])]
+    stores[0].start()
     out_high, out_low = split(w_out[...])
     out_high = out_high.astype(F32)
     out_low = out_low.astype(F32)
-    chan = w_out.shape[0]
     stack = jnp.concatenate([out_high, out_low, jnp.zeros((128 - 2 * chan, hid), F32)], axis=0)
     wo_f[...] = stack.T.astype(BF16)
     wo_b[...] = jnp.concatenate(
         [out_high, out_low, out_high, jnp.zeros((128 - 3 * chan, hid), F32)], axis=0
     ).astype(BF16)
+    for r in range(rows):
+        loads[r].wait()
+        block = columns[r].T
+        for half in range(2):
+            turned[half, r * cols : (r + 1) * cols, :] = block[:, half * 128 : half * 128 + 128]
+            store = pltpu.make_async_copy(
+                turned.at[half, pl.ds(r * cols, cols), :],
+                s_out.at[pl.ds(r * cols, cols), half, :],
+                out_sems.at[r, half],
+            )
+            store.start()
+            stores.append(store)
+    load_mid.wait()
+    wm_v[0], wm_v[1] = split(w_mid[...])
+    stores.append(pltpu.make_async_copy(wm_v, wm, sems.at[2]))
+    stores[-1].start()
+    for store in stores:
+        store.wait()
 
 
 def forward_kernel(
-    recv, s0_hbm, s1_hbm, wi_hbm, wm_hbm, wo_hbm, b_in, b_mid,
+    recv, s0_hbm, wi_hbm, wm_hbm, wo_hbm, b_in, b_mid,
     h1_out, h2_out, r_out, cell_out, send,
-    s0, s1, wi, wm, wo, g0, g1, q, w, p, z, moments, cell_smem, sems,
+    s0, wi, wm, wo, g0, q, w, p, z, moments, cell_smem, sems,
 ):
     step = pl.program_id(0)
-    peers = recv.shape[0] // 8
+    peers = recv.shape[0] // ASK
     blocks = peers // 8
 
     def fetch(row, to_row):
-        g0[pl.ds(to_row, 1), :] = s0[pl.ds(row, 1), :]
-        g1[pl.ds(to_row, 1), :] = s1[pl.ds(row, 1), :]
+        g0[to_row] = s0[row]
 
     @pl.when(step == 0)
     def _():
         copies = [
             pltpu.make_async_copy(source, target, sems.at[i])
             for i, (source, target) in enumerate(
-                ((s0_hbm, s0), (s1_hbm, s1), (wi_hbm, wi), (wm_hbm, wm), (wo_hbm, wo))
+                ((s0_hbm, s0), (wi_hbm, wi), (wm_hbm, wm), (wo_hbm, wo))
             )
         ]
         for copy in copies:
             copy.start()
-        packed = jnp.concatenate([recv[pl.ds(a, peers, stride=8), :] for a in range(6)], axis=0)
+        packed = jnp.concatenate([recv[pl.ds(a, peers, stride=ASK), :] for a in range(ASK)], axis=0)
         tiles = swap_groups(packed)
 
         def tile(a, i):
@@ -148,31 +182,37 @@
         moments[...] = jnp.zeros_like(moments)
         copy.wait()
         copies[0].wait()
-        copies[1].wait()
 
         def gather(i, carry):
             for k in range(GROUP):
                 fetch(cell_smem[i // 8, (i % 8) * GROUP + k], i * GROUP + k)
             return carry
 
-        lax.fori_loop(0, TILE // GROUP, gather, 0)
-        for copy in copies[2:]:
+        for n in range(TILE):
+            fetch(cell_smem[n // LANES, n % LANES], n)
+        for copy in copies[1:]:
             copy.wait()
 
     start = pl.multiple_of(step * TILE, TILE)
     here = pl.ds(start, TILE)
-    high, low = split(jnp.concatenate([g0[here, :], g1[here, :]], axis=1))
+    high, low = split(jnp.concatenate([g0[here, 0, :], g0[here, 1, :]], axis=1))
+    parts = [slice(j * TILE // 2, (j + 1) * TILE // 2) for j in range(2)]
+    h1s = []
+    for s in parts:
+        h1 = jnp.tanh(mm3((high[s], low[s]), wi) + b_in[...][None, :])
+        h1_out[s, :] = h1
+        h1s.append(split(h1))
     following = jnp.minimum(step + 1, pl.num_programs(0) - 1)
     for n in range(TILE):
         fetch(
             cell_smem[following * (TILE // LANES) + n // LANES, n % LANES], following * TILE + n
         )
-    h1 = jnp.tanh(mm3_of(high, low, wi[0], wi[1]) + b_in[...][None, :])
-    h1_out[...] = h1
-    h2 = jnp.tanh(mm3(h1, wm[0], wm[1]) + b_mid[...][None, :])
-    h2_out[...] = h2
-    high, low = split(h2)
-    total = (mm(high, wo[...]) + mm(low, wo[...])).T
+    h2s = []
+    for s, hl in zip(parts, h1s):
+        h2 = jnp.tanh(mm3_turned(hl, wm) + b_mid[...][None, :])
+        h2_out[s, :] = h2
+        h2s.append(split(h2))
+    total = jnp.concatenate([mm(jnp.concatenate(hl,axis=1), jnp.concatenate([wo[...],wo[...]],axis=0)) for hl in h2s], axis=0).T
     zt = total[0:16] + total[16:32]
     z[:, here] = zt
     residual = w[:, here] * (zt - q[:, here])
@@ -190,12 +230,12 @@
     @pl.when(step == pl.num_programs(0) - 1)
     def _():
         packed = swap_groups(to_tiles([z[0:8, :], z[8:16, :]]))
-        send[pl.ds(0, peers, stride=8), :] = packed[:peers]
-        send[pl.ds(1, peers, stride=8), :] = packed[peers:]
+        send[pl.ds(0, peers, stride=REPLY), :] = packed[:peers]
+        send[pl.ds(1, peers, stride=REPLY), :] = packed[peers:]
         lane_group = lax.broadcasted_iota(jnp.int32, (8, LANES), 1) // GROUP
         own = lane_group == lax.broadcasted_iota(jnp.int32, (8, LANES), 0)
         row = jnp.sum(jnp.where(own, moments[...], 0.0), axis=0, keepdims=True)
-        send[pl.ds(2, peers, stride=8), :] = jnp.broadcast_to(row, (peers, LANES))
+        send[pl.ds(2, peers, stride=REPLY), :] = jnp.broadcast_to(row, (peers, LANES))
 
 
 def backward_kernel(
@@ -251,9 +291,9 @@
     ins = []
     for s, back_mid in zip(halves, mids):
         x1 = h1[pl.ds(start + s.start, TILE // 2), :]
-        ins.append(mm3(back_mid, wm[0], wm[1]) * (1.0 - x1 * x1))
+        ins.append(mm3(split(back_mid), wm) * (1.0 - x1 * x1))
     for s, back_in in zip(halves, ins):
-        increment = mm3(back_in, wi[0], wi[1])
+        increment = mm3_turned(split(back_in), wi)
         i0[s, :] = increment[:, :128]
         i1[s, :] = increment[:, 128:]
 
@@ -266,7 +306,9 @@
                 add(cells[row, at], cells[row, at + 1], i * GROUP + k)
             return carry
 
-        lax.fori_loop(0, TILE // GROUP, scatter, 0)
+        for n in range(0, TILE, 2):
+            row = last * (TILE // LANES) + n // LANES
+            add(cells[row, n % LANES], cells[row, n % LANES + 1], n)
         feat, rows, cols = grad.shape
         copies = []
         for row in range(rows):
@@ -284,7 +326,7 @@
     used = jnp.where(used_slots(count), 1.0, 0.0)
     tiles = swap_groups(
         jnp.concatenate(
-            [recv[pl.ds(0, peers, stride=8), :], recv[pl.ds(1, peers, stride=8), :], used], axis=0
+            [recv[pl.ds(0, peers, stride=REPLY), :], recv[pl.ds(1, peers, stride=REPLY), :], used], axis=0
         )
     )
     blocks = peers // 8
@@ -295,7 +337,7 @@
             value = tiles[(a * blocks + i) * 8 : (a * blocks + i) * 8 + 8]
             rows = slice(8 * a, 8 * a + 8)
             evolved[rows, lanes] = jnp.where(keep, value + base[rows, lanes], 0.0)
-    row = jnp.sum(recv[pl.ds(2, peers, stride=8), :], axis=0, keepdims=True)
+    row = jnp.sum(recv[pl.ds(2, peers, stride=REPLY), :], axis=0, keepdims=True)
     lane = lax.broadcasted_iota(jnp.int32, (8, LANES), 1)
     spread = jnp.where(
         lane // GROUP == lax.broadcasted_iota(jnp.int32, (8, LANES), 0),
@@ -323,9 +365,9 @@
 
 
 def exchange(data, peers):
-    blocks = data.reshape(peers, 8, LANES)
-    blocks = lax.all_to_all(blocks, ("gx", "gy"), split_axis=0, concat_axis=0, tiled=True)
-    return blocks.reshape(peers * 8, LANES)
+    parts = data.reshape(peers, 1, -1)
+    parts = lax.all_to_all(parts, ("gx", "gy"), split_axis=0, concat_axis=0, tiled=True)
+    return parts.reshape(data.shape)
 
 
 def per_device(
@@ -339,32 +381,41 @@
     cells = rows * cols
     send, base = pl.pallas_call(
         request_kernel,
-        out_shape=(shape((peers * 8, LANES)), shape((16, slots))),
+        out_shape=(shape((peers * ASK, LANES)), shape((16, slots))),
         name="request",
     )(obs_cell, obs_count, obs_value, obs_weight, predictor, bias_coef.T, bias_out[None, :])
     recv = exchange(send, peers)
-    s0, s1, wi_f, wi_b, wm_f, wm_b, wo_f, wo_b = pl.pallas_call(
+    in_hbm = pl.BlockSpec(memory_space=pltpu.HBM)
+    in_vmem = pl.BlockSpec(memory_space=pltpu.VMEM)
+    s0, wi, wm, wo_f, wo_b = pl.pallas_call(
         prepare_kernel,
+        in_specs=[in_hbm, in_vmem, in_hbm, in_vmem],
+        out_specs=[in_hbm, in_hbm, in_hbm, in_vmem, in_vmem],
         out_shape=(
-            shape((cells, 128)), shape((cells, 128)),
-            shape((2, 256, hid), BF16), shape((2, hid, 256), BF16),
-            shape((2, hid, hid), BF16), shape((2, hid, hid), BF16),
+            shape((cells, 2, 128)),
+            shape((2, 256, hid), BF16), shape((2, hid, hid), BF16),
             shape((hid, 128), BF16), shape((128, hid), BF16),
         ),
+        scratch_shapes=[
+            pltpu.VMEM((rows, 256, cols), F32), pltpu.VMEM((2, cells, 128), F32),
+            pltpu.VMEM((hid, hid), F32),
+            pltpu.VMEM((2, 256, hid), BF16), pltpu.VMEM((2, hid, hid), BF16),
+            pltpu.SemaphoreType.DMA((3,)), pltpu.SemaphoreType.DMA((rows,)),
+            pltpu.SemaphoreType.DMA((rows, 2)),
+        ],
         name="prepare",
         cost_estimate=pl.CostEstimate(flops=10**7, transcendentals=0, bytes_accessed=15 * 10**6),
-    )(model_state.reshape(feat * rows, cols), weight_in.T, weight_mid, weight_out)
+    )(model_state, weight_in.T, weight_mid, weight_out)
 
     def whole(dims):
         return pl.BlockSpec(dims, lambda i: (0,) * len(dims))
 
     steps = slots // TILE
-    in_hbm = pl.BlockSpec(memory_space=pltpu.HBM)
     h1, h2, residual, cell, reply = pl.pallas_call(
         forward_kernel,
         grid=(steps,),
         in_specs=[
-            whole((peers * 8, LANES)), in_hbm, in_hbm, in_hbm, in_hbm, in_hbm,
+            whole((peers * ASK, LANES)), in_hbm, in_hbm, in_hbm, in_hbm,
             whole((hid,)), whole((hid,)),
         ],
         out_specs=[
@@ -372,17 +423,17 @@
             pl.BlockSpec((TILE, hid), lambda i: (i, 0)),
             pl.BlockSpec((TILE, 128), lambda i: (i, 0)),
             whole((slots // LANES, LANES)),
-            whole((peers * 8, LANES)),
+            whole((peers * REPLY, LANES)),
         ],
         out_shape=(
             shape((slots, hid)), shape((slots, hid)), shape((slots, 128), BF16),
-            shape((slots // LANES, LANES), jnp.int32), shape((peers * 8, LANES)),
+            shape((slots // LANES, LANES), jnp.int32), shape((peers * REPLY, LANES)),
         ),
         scratch_shapes=[
-            pltpu.VMEM((cells, 128), F32), pltpu.VMEM((cells, 128), F32),
+            pltpu.VMEM((cells, 2, 128), F32),
             pltpu.VMEM((2, 256, hid), BF16), pltpu.VMEM((2, hid, hid), BF16),
             pltpu.VMEM((hid, 128), BF16),
-            pltpu.VMEM((slots, 128), F32), pltpu.VMEM((slots, 128), F32),
+            pltpu.VMEM((slots, 2, 128), F32),
             pltpu.VMEM((16, slots), F32), pltpu.VMEM((16, slots), F32),
             pltpu.VMEM((8, slots), F32), pltpu.VMEM((16, slots), F32),
             pltpu.VMEM((8, LANES), F32),
@@ -395,7 +446,7 @@
             flops=6 * slots * hid * (256 + hid + 128), transcendentals=2 * slots * hid,
             bytes_accessed=25 * 10**6,
         ),
-    )(recv, *map(stay, (s0, s1, wi_f, wm_f, wo_f)), bias_in, bias_mid)
+    )(recv, *map(stay, (s0, wi, wm, wo_f)), bias_in, bias_mid)
     back = exchange(reply, peers)
     gradient = pl.pallas_call(
         backward_kernel,
@@ -411,7 +462,7 @@
         scratch_shapes=[
             pltpu.VMEM((slots, hid), F32), pltpu.VMEM((slots, hid), F32),
             pltpu.VMEM((128, hid), BF16), pltpu.VMEM((2, hid, hid), BF16),
-            pltpu.VMEM((2, hid, 256), BF16),
+            pltpu.VMEM((2, 256, hid), BF16),
             pltpu.VMEM((TILE, 128), F32), pltpu.VMEM((TILE, 128), F32),
         ]
         + [pltpu.VMEM((cells, 128), F32) for _ in range(4)]
@@ -425,7 +476,7 @@
             flops=6 * slots * hid * (256 + hid + 128), transcendentals=0,
             bytes_accessed=25 * 10**6,
         ),
-    )(cell, h1, h2, residual, wo_b, wm_b, wi_b)
+    )(cell, h1, h2, residual, wo_b, wm, wi)
     evolved, bias_gradient = pl.pallas_call(
         finish_kernel,
         out_shape=(shape((16, slots)), shape((8, 16))),

time: 81.8 us -> 76.6 us (0.936)
  Pallas kernels: 59.5 us -> 54.3 us
    pallas_call x3, Pallas kernels: 36.1 us -> 31.3 us  [the longest x1 19.6 us: per_device(): pl.pallas_call(forward_kernel, grid=(steps,), in_specs=[whole((peers * AS...]
  transfers between devices with their start and end apart: 2 -> 2, of which waited for: 1 -> 1; matrix products, arithmetic and copies ran while one was open for 0% -> 0% of each run, Pallas kernels for 39% -> 41%
where the time goes in v3:
time: 76.6 us; the launch traced here: 76.3 us
  Pallas kernels  54.3 us (71%)
  starting transfers between devices  17.6 us (23%)
  waiting for transfers between devices  3.67 us (5%)
    pallas_call x1, Pallas kernels, per_device(): pl.pallas_call(backward_kernel, grid=(steps,), in_specs=[pl.BlockSpec(mem...  21.9 us
    pallas_call x1, Pallas kernels, per_device(): pl.pallas_call(forward_kernel, grid=(steps,), in_specs=[whole((peers * AS...  19.6 us
    all_to_all x2, starting transfers between devices, exchange(): lax.all_to_all(parts, ('gx', 'gy'), split_axis=0, concat_axis=0, tiled=True)  17.6 us
    pallas_call x1, Pallas kernels, per_device(): pl.pallas_call(prepare_kernel, in_specs=[in_hbm, in_vmem, in_hbm, in_vmem...  9.07 us
    all_to_all x2, waiting for transfers between devices, exchange(): lax.all_to_all(parts, ('gx', 'gy'), split_axis=0, concat_axis=0, tiled=True)  3.67 us
    pallas_call x1, Pallas kernels, per_device(): pl.pallas_call(request_kernel, out_shape=(shape((peers * ASK, LANES)), sh...  2.57 us
  transfers between devices with their start and end apart: 2, of which 1 were waited for; matrix products, arithmetic and copies ran while one was open for 0% of the time, Pallas kernels for 41%

profile of v3, /device:TPU:1, one launch (start us, length us, event | category | flops | bytes accessed | tf_op | source)
XLA Modules:
  0.0 76.3 jit_solution(3494281085135004537)
XLA Ops:
  0.6 2.6 %request.1 = (f32[768,128]{1,0:T(8,128)}, f32[16,2048]{1,0:T(8,128)}) custom-call(s32[1,2048]{1,0:T(1,128)} %cell.1, s32[1,128]{1,0:T(1,128)} %count.3, f32[16,2048]{1,0:T(8,128)} %obs.1, f32[16,2048]{1,0:T(8,128)} %weight.1, f32[8,2048]{1,0:T(8,128)} %pred_.1, f32[8,16]{1,0:T(8,128)} %bitcast.13, f32[1,16]{1,0:T(1,128)} %bitcast.14), custom_call_target="tpu_custom_call" | custom-call | tf_op jit(solution)/shard_map/request/pallas_call | solution.py:382
  3.2 11.5 %all-to-all-start = ((f32[128,1,768]{2,1,0:T(1,128)}), f32[128,1,768]{2,1,0:T(1,128)S(1)}, u32[]{:S(2)}, u32[]{:S(2)}) async-start(f32[128,1,768]{2,1,0:T(1,128)} %bitcast.11), calls=%async_computation | async-start | bytes 786432 | tf_op jit(solution)/shard_map/all_to_all | solution.py:369
  14.7 0.0 copy-start.2
  14.7 0.0 copy-start.3
  14.7 9.1 %prepare.1 = (f32[4096,2,128]{2,1,0:T(2,128)}, bf16[2,256,768]{2,1,0:T(8,128)(2,1)}, bf16[2,768,768]{2,1,0:T(8,128)(2,1)}, bf16[768,128]{1,0:T(8,128)(2,1)}, bf16[128,768]{1,0:T(8,128)(2,1)}) custom-call(f32[200,32,128]{2,1,0:T(8,128)} %state.1, f32[200,768]{1,0:T(8,128)} %bitcast.10, f32[768,768]{1,0:T(8,128)} %w_mid_hbm.1, f32[16,768]{1,0:T(8,128)} %w_out.1), custom_call_target="tpu_custom_call" | custom-call | flops 10000000 | bytes 15000000 | tf_op jit(solution)/shard_map/prepare/pallas_call | solution.py:390
  23.8 3.7 %all-to-all-done = f32[128,1,768]{2,1,0:T(1,128)S(1)} async-done(((f32[128,1,768]{2,1,0:T(1,128)}), f32[128,1,768]{2,1,0:T(1,128)S(1)}, u32[]{:S(2)}, u32[]{:S(2)}) %all-to-all-start) | async-done | bytes 393248 | tf_op jit(solution)/shard_map/all_to_all | solution.py:369
  27.5 0.0 copy-done.2
  27.5 0.0 copy-done.3
  27.5 19.6 %forward.1 = (f32[2048,768]{1,0:T(8,128)}, f32[2048,768]{1,0:T(8,128)}, bf16[2048,128]{1,0:T(8,128)(2,1)}, s32[16,128]{1,0:T(8,128)}, f32[384,128]{1,0:T(8,128)}) custom-call(f32[768,128]{1,0:T(8,128)S(1)} %bitcast.9, f32[4096,2,128]{2,1,0:T(2,128)} %get-tuple-element.18.s0_hbm, bf16[2,256,768]{2,1,0:T(8,128)(2,1)} %get-tuple-element.19.wi_hbm, ...), custom_call_target="tpu_custom_call" | custom-call | flops 10871635968 | bytes 25000000 | tf_op jit(solution)/shard_map/forward/pallas_call | solution.py:414
  47.1 6.1 %all-to-all-start.1 = ((f32[128,1,384]{2,1,0:T(1,128)}), f32[128,1,384]{2,1,0:T(1,128)S(1)}, u32[]{:S(2)}, u32[]{:S(2)}) async-start(f32[128,1,384]{2,1,0:T(1,128)} %bitcast.12), calls=%async_computation.1 | async-start | bytes 393216 | tf_op jit(solution)/shard_map/all_to_all | solution.py:369
  53.3 0.0 copy-start
  53.3 0.0 copy-start.1
  53.3 21.9 %backward.1 = f32[200,32,128]{2,1,0:T(8,128)} custom-call(s32[16,128]{1,0:T(8,128)} %get-tuple-element.22.cells, f32[2048,768]{1,0:T(8,128)} %get-tuple-element.23.h1_hbm, f32[2048,768]{1,0:T(8,128)} %get-tuple-element.24.h2_hbm, bf16[2048,128]{1,0:T(8,128)(2,1)} %get-tuple-element.25.r, bf16[128,768]{1,0:T(8,128)(2,1)} %get-tuple-element.26.wo_hbm, ...), custom_call_target="tpu_custom_call" | custom-call | flops 10871635968 | bytes 25000000 | tf_op jit(solution)/shard_map/backward/pallas_call | solution.py:451
  75.2 0.0 all-to-all-done.1
  75.2 0.0 copy-done
  75.2 0.0 copy-done.1
  75.2 1.1 %finish.1 = (f32[16,2048]{1,0:T(8,128)}, f32[8,16]{1,0:T(8,128)}) custom-call(f32[384,128]{1,0:T(8,128)S(1)} %bitcast.8, f32[16,2048]{1,0:T(8,128)S(1)} %copy-done, s32[1,128]{1,0:T(1,128)S(1)} %copy-done.1), custom_call_target="tpu_custom_call" | custom-call | tf_op jit(solution)/shard_map/finish/pallas_call | solution.py:480
Async XLA Ops:
  3.2 24.3 %all-to-all-start = ((f32[128,1,768]{2,1,0:T(1,128)}), f32[128,1,768]{2,1,0:T(1,128)S(1)}, u32[]{:S(2)}, u32[]{:S(2)}) async-start(f32[128,1,768]{2,1,0:T(1,128)} %bitcast.11), calls=%async_computation | async-start | bytes 786432 | tf_op jit(solution)/shard_map/all_to_all | solution.py:369
  14.7 12.8 %copy-start.2 = (f32[768]{0:T(1024)S(1)}, f32[768]{0:T(1024)}, u32[]{:S(2)}) copy-start(f32[768]{0:T(1024)} %b_in.1) | copy-start | bytes 9220
  14.7 12.8 %copy-start.3 = (f32[768]{0:T(1024)S(1)}, f32[768]{0:T(1024)}, u32[]{:S(2)}) copy-start(f32[768]{0:T(1024)} %b_mid.1) | copy-start | bytes 9220
  47.1 28.1 %all-to-all-start.1 = ((f32[128,1,384]{2,1,0:T(1,128)}), f32[128,1,384]{2,1,0:T(1,128)S(1)}, u32[]{:S(2)}, u32[]{:S(2)}) async-start(f32[128,1,384]{2,1,0:T(1,128)} %bitcast.12), calls=%async_computation.1 | async-start | bytes 393216 | tf_op jit(solution)/shard_map/all_to_all | solution.py:369
  53.3 22.0 %copy-start = (f32[16,2048]{1,0:T(8,128)S(1)}, f32[16,2048]{1,0:T(8,128)}, u32[]{:S(2)}) copy-start(f32[16,2048]{1,0:T(8,128)} %get-tuple-element.28.base) | copy-start | bytes 393220
  53.3 22.0 %copy-start.1 = (s32[1,128]{1,0:T(1,128)S(1)}, s32[1,128]{1,0:T(1,128)}, u32[]{:S(2)}) copy-start(s32[1,128]{1,0:T(1,128)} %count.3) | copy-start | bytes 1540
